TPU v7x, 512 devices: a whole 4x8x8 slice. The times are simulated.
512 devices in a mesh: sp: 64 (over z_hi, y, core), ch: 8 (over z_lo, x).
Axes of the slice: x: 4, y: 8, z: 8 (z_hi: 4, z_lo: 2; z = z_hi * 2 + z_lo), core: 2. Of those that a mesh axis runs over, the one named last changes fastest.
Arguments:
- image: bfloat16 [64, 4, 64, 768], P('sp', None, None, 'ch'), may hold values from -60 to 60
- cotangent: bfloat16 [64, 4, 64, 768], P('sp', None, None, 'ch'), may hold values from -6 to 6
- kernel: bfloat16 [7, 7, 768], P(None, None, 'ch'), may hold values from -0.875 to 0.875
- w_in: bfloat16 [768, 3072], P(None, 'ch'), may hold values from -0.21875 to 0.21875
- w_out: bfloat16 [3072, 768], P('ch'), may hold values from -0.109375 to 0.109375
Outputs:
- output: bfloat16 [64, 4, 64, 768], P('sp', None, None, 'ch')
- grad_image: bfloat16 [64, 4, 64, 768], P('sp', None, None, 'ch')
- grad_in: float32 [768, 3072], P(None, 'ch')
- grad_out: float32 [3072, 768], P('ch')
- grad_kernel: float32 [7, 7, 768], P(None, None, 'ch')
All inputs are finite; a program needn't handle non-finite values.
Results may differ from a plain program's by a relative error of at most 0.015.
Values may be sent and summed in bfloat16 or wider, within the bound.
A program may use at most 64 MiB of HBM per device.

v0:
```python
import jax
import jax.numpy as jnp
from jax import lax
from jax.sharding import PartitionSpec as P

GRID_W = 8


def passed_along(block, axis, distance):
    devices = range(lax.axis_size(axis))
    route = [(i - distance, i) for i in devices if i - distance in devices]
    return lax.ppermute(block, axis, route)


def from_peer(piece, offset):
    return passed_along(piece, "sp", offset)


def widen(block):
    column = lax.axis_index("sp") % GRID_W
    left = from_peer(block[:, -3:], 1)
    left = jnp.where(column == 0, jnp.zeros_like(left), left)
    right = from_peer(block[:, :3], -1)
    right = jnp.where(column == GRID_W - 1, jnp.zeros_like(right), right)
    wide = jnp.concatenate([left, block, right], axis=1)
    upper = from_peer(wide[-3:], GRID_W)
    lower = from_peer(wide[:3], -GRID_W)
    return jnp.concatenate([upper, wide, lower], axis=0)


def shards(image, cotangent, kernel, w_in, w_out):
    block = image[0]
    grad_map = cotangent[0]
    rows, cols, panel = block.shape
    chans = w_in.shape[0]
    kernel_f = kernel.astype(jnp.float32)
    padded = widen(block).astype(jnp.float32)
    total = jnp.zeros((rows, cols, panel), jnp.float32)
    for row in range(7):
        for col in range(7):
            total = total + kernel_f[row, col] * padded[row : row + rows, col : col + cols]
    conv = total.astype(jnp.bfloat16)
    conv_f = conv.astype(jnp.float32)
    first_sum, square_sum = lax.psum(
        (jnp.sum(conv_f, axis=-1, keepdims=True), jnp.sum(conv_f * conv_f, axis=-1, keepdims=True)),
        "ch",
    )
    mean = first_sum / chans
    var = square_sum / chans - mean * mean
    rstd = lax.rsqrt(var + 1e-06)
    normed_all = lax.all_gather(
        ((conv_f - mean) * rstd).astype(jnp.bfloat16), "ch", axis=2, tiled=True
    )
    local_hat = (conv_f - mean) * rstd
    pre = jnp.einsum("hwc,cf->hwf", normed_all, w_in, preferred_element_type=jnp.float32)
    act = (0.5 * pre * (1.0 + jax.scipy.special.erf(pre / jnp.sqrt(2.0)))).astype(jnp.bfloat16)
    partial_out = jnp.einsum("hwf,fc->hwc", act, w_out, preferred_element_type=jnp.float32).astype(
        jnp.bfloat16
    )
    branch = lax.psum_scatter(partial_out, "ch", scatter_dimension=2, tiled=True).astype(
        jnp.float32
    )
    output = (block.astype(jnp.float32) + branch).astype(jnp.bfloat16)
    grad_all = lax.all_gather(grad_map, "ch", axis=2, tiled=True)
    d_act = jnp.einsum("hwc,fc->hwf", grad_all, w_out, preferred_element_type=jnp.float32)
    grad_out = jnp.einsum("hwf,hwc->fc", act, grad_all, preferred_element_type=jnp.float32)
    slope = 0.5 * (1.0 + jax.scipy.special.erf(pre / jnp.sqrt(2.0))) + pre * jnp.exp(
        -0.5 * pre * pre
    ) / jnp.sqrt(2.0 * jnp.pi)
    d_pre = (d_act * slope).astype(jnp.bfloat16)
    grad_in = jnp.einsum("hwc,hwf->cf", normed_all, d_pre, preferred_element_type=jnp.float32)
    partial_norm = jnp.einsum(
        "hwf,cf->hwc", d_pre, w_in, preferred_element_type=jnp.float32
    ).astype(jnp.bfloat16)
    d_norm = lax.psum_scatter(partial_norm, "ch", scatter_dimension=2, tiled=True).astype(
        jnp.float32
    )
    first, second = lax.psum(
        (
            jnp.sum(d_norm, axis=-1, keepdims=True),
            jnp.sum(d_norm * local_hat, axis=-1, keepdims=True),
        ),
        "ch",
    )
    d_conv = (rstd * (d_norm - first / chans - local_hat * second / chans)).astype(jnp.bfloat16)
    d_conv_f = d_conv.astype(jnp.float32)
    taps = []
    for row in range(7):
        for col in range(7):
            taps.append(jnp.sum(d_conv_f * padded[row : row + rows, col : col + cols], axis=(0, 1)))
    grad_kernel = jnp.stack(taps).reshape(7, 7, panel)
    d_padded = widen(d_conv).astype(jnp.float32)
    back = grad_map.astype(jnp.float32)
    for row in range(7):
        for col in range(7):
            back = (
                back
                + kernel_f[row, col] * d_padded[6 - row : 6 - row + rows, 6 - col : 6 - col + cols]
            )
    grad_image = back.astype(jnp.bfloat16)
    grad_in, grad_out, grad_kernel = lax.psum((grad_in, grad_out, grad_kernel), "sp")
    return (output[None], grad_image[None], grad_in, grad_out, grad_kernel)


def solution(mesh):
    return jax.shard_map(
        shards,
        mesh=mesh,
        in_specs=(
            P("sp", None, None, "ch"),
            P("sp", None, None, "ch"),
            P(None, None, "ch"),
            P(None, "ch"),
            P("ch", None),
        ),
        out_specs=(
            P("sp", None, None, "ch"),
            P("sp", None, None, "ch"),
            P(None, "ch"),
            P("ch", None),
            P(None, None, "ch"),
        ),
        check_vma=False,
    )
```

profile of v0, /device:TPU:1, one launch (start us, length us, event | category | flops | bytes accessed | tf_op | source)
XLA Modules:
  0.0 714.7 jit_solution(15601981577770408222)
XLA Ops:
  9.2 4.6 collective-permute-start
  13.8 5.5 collective-permute-start.1
  22.4 4.2 collective-permute-start.2
  26.6 1.3 collective-permute-start.3
  27.9 25.2 %all-gather = bf16[1,4,64,768]{2,1,0,3:T(4,128)(2,1)S(1)} all-gather(bf16[1,4,64,96]{2,1,0,3:T(4,128)(2,1)S(1)} %copy.42), channel_id=2, replica_groups=mesh['sp'=64,'ch'=8] {'ch'}, dimensions={3}, use_global_device_ids=true | all-gather | bytes 442368 | tf_op jit(solution)/shard_map/all_gather | solution.py:64
  54.8 12.5 %convert_reduce_fusion.1 = (f32[4,64]{1,0:T(4,128)S(1)}, f32[4,64]{1,0:T(4,128)S(1)}, bf16[4,64,96]{1,0,2:T(4,128)(2,1)S(1)}) fusion(f32[10,70,96]{1,0,2:T(8,128)S(1)} %maximum_convert_fusion, f32[96]{0:T(128)S(1)} %get-tuple-element.90, f32[96]{0:T(128)S(1)} %get-tuple-element.91, f32[96]{0:T(128)S(1)} %get-tuple-element.92, f32[96]{0:T(128)S(1)} %get-tuple-element.93, ...), kind=kLoop, calls=%fused_computation.76 | loop fusion | flops 2506240 | bytes 4886912 | tf_op jit(solution)/shard_map/reduce_sum | solution.py:45
  67.3 16.1 %all-reduce.2 = (f32[4,64,1]{1,0,2:T(4,128)S(1)}, f32[4,64,1]{1,0,2:T(4,128)S(1)}) all-reduce(f32[4,64,1]{1,0,2:T(4,128)S(1)} %bitcast.206, f32[4,64,1]{1,0,2:T(4,128)S(1)} %bitcast.205), channel_id=1, replica_groups=mesh['sp'=64,'ch'=8] {'ch'}, use_global_device_ids=true, to_apply=%region_3.4 | all-reduce | flops 512 | bytes 4096 | tf_op jit(solution)/shard_map/psum | solution.py:44
  83.5 24.4 %all_gather.6 = bf16[4,64,768]{1,0,2:T(4,128)(2,1)S(1)} all-gather(bf16[4,64,96]{1,0,2:T(4,128)(2,1)S(1)} %fusion.14), channel_id=1, replica_groups=mesh['sp'=64,'ch'=8] {'ch'}, dimensions={2}, use_global_device_ids=true | all-gather | bytes 442368 | tf_op jit(solution)/shard_map/all_gather | solution.py:51
  112.9 1.4 convolution_convert_fusion.1
  116.4 1.4 convolution_bitcast_fusion.1
  117.8 1.4 convolution_bitcast_fusion
  119.3 51.6 %reduce-scatter.9.cloned.1.call-done = bf16[96,256]{1,0:T(8,128)(2,1)} async-done(((bf16[768,256]{1,0:T(8,128)(2,1)}), bf16[96,256]{1,0:T(8,128)(2,1)}) %reduce-scatter.9.cloned.1.call-update) | async-done | bytes 49168
  171.9 14.9 %all-reduce.1 = (f32[4,64]{1,0:T(4,128)S(1)}, f32[4,64,1]{1,0,2:T(4,128)S(1)}) all-reduce(f32[4,64]{1,0:T(4,128)S(1)} %get-tuple-element.70, f32[4,64,1]{1,0,2:T(4,128)S(1)} %bitcast.204), channel_id=1, replica_groups=mesh['sp'=64,'ch'=8] {'ch'}, use_global_device_ids=true, to_apply=%region_9.10 | all-reduce | flops 512 | bytes 4096 | tf_op jit(solution)/shard_map/psum | solution.py:78
  186.8 6.9 fusion.68
  193.7 4.6 fusion.67
  198.5 10.8 %collective-permute-start.4 = (bf16[4,3,96]{1,0,2:T(4,128)(2,1)S(1)}, bf16[4,3,96]{1,0,2:T(4,128)(2,1)S(1)}, u32[]{:S(2)}, u32[]{:S(2)}) collective-permute-start(bf16[4,3,96]{1,0,2:T(4,128)(2,1)S(1)} %get-tuple-element.83), channel_id=1, source_target_pairs={{0,8},{8,16},{16,24},{24,32},{32,40},{40,48},{48,56},{56,64},{64,7... | collective-permute-start | bytes 6920 | tf_op jit(solution)/shard_map/ppermute | solution.py:12
  209.3 6.7 fusion.69
  216.0 1.9 collective-permute-start.5
  218.9 3.4 collective-permute-done.5
  223.0 6.0 collective-permute-start.6
  231.3 277.0 %psum.55 = f32[7,7,96]{2,1,0:T(8,128)} all-reduce(f32[7,7,96]{2,1,0:T(8,128)S(1)} %reshape.13), channel_id=1, replica_groups=mesh['sp'=64,'ch'=8] {'sp'}, use_global_device_ids=true, to_apply=%region_61.62 | all-reduce | flops 4704 | bytes 37632 | tf_op jit(solution)/shard_map/psum | solution.py:101
  509.3 12.5 %fusion.121 = bf16[1,4,64,96]{2,1,3,0:T(4,128)(2,1)S(1)} fusion(f32[10,70,96]{1,0,2:T(8,128)S(1)} %maximum_convert_fusion.1, f32[96]{0:T(128)S(1)} %copy-done.45, f32[96]{0:T(128)S(1)} %copy-done.47, f32[96]{0:T(128)S(1)} %copy-done.49, f32[96]{0:T(128)S(1)} %copy-done.51, f32[96]{0:T(128)S(1)} %copy-done.53, f32[96]{0:T(128)S(1)} %copy-done.55, ...), kind=kLoop, calls=%fused_computation.243 | loop fusion | flops 2457600 | bytes 4934016 | tf_op jit(solution)/shard_map/broadcast_in_dim | solution.py:102
  522.6 181.2 %all-reduce.5.cloned.1.call-done = (f32[768,384]{1,0:T(8,128)}, f32[384,768]{1,0:T(8,128)}) async-done(((f32[768,384]{1,0:T(8,128)}, f32[384,768]{1,0:T(8,128)}), (f32[768,384]{1,0:T(8,128)}, f32[384,768]{1,0:T(8,128)})) %all-reduce.5.cloned.1.call-update) | async-done | bytes 2359312 | tf_op jit(solution)/shard_map/psum | solution.py:101
  703.8 2.5 copy.54
  (223 shorter events, 19.5 us)
Async XLA Ops:
  8.0 162.9 %reduce-scatter.9.cloned.1.call-start = ((), (), s32[]{:S(2)}) async-start(), calls=%async_computation.3 | async-start | bytes 442368
  9.2 12.8 %collective-permute-start = (bf16[4,3,96]{1,0,2:T(4,128)(2,1)S(1)}, bf16[4,3,96]{1,0,2:T(4,128)(2,1)S(1)}, u32[]{:S(2)}, u32[]{:S(2)}) collective-permute-start(bf16[4,3,96]{1,0,2:T(4,128)(2,1)S(1)} %get-tuple-element.87), channel_id=1, source_target_pairs={{0,8},{8,16},{16,24},{24,32},{32,40},{40,48},{48,56},{56,64},{64,7... | collective-permute-start | bytes 6920 | tf_op jit(solution)/shard_map/ppermute | solution.py:12
  13.8 8.2 %collective-permute-start.1 = (bf16[4,3,96]{1,0,2:T(4,128)(2,1)S(1)}, bf16[4,3,96]{1,0,2:T(4,128)(2,1)S(1)}, u32[]{:S(2)}, u32[]{:S(2)}) collective-permute-start(bf16[4,3,96]{1,0,2:T(4,128)(2,1)S(1)} %get-tuple-element.88), channel_id=1, source_target_pairs={{8,0},{16,8},{24,16},{32,24},{40,32},{48,40},{56,48},{64,56},{72,6... | collective-permute-start | bytes 6920 | tf_op jit(solution)/shard_map/ppermute | solution.py:12
  22.4 31.3 %collective-permute-start.2 = (bf16[3,70,96]{1,0,2:T(4,128)(2,1)S(1)}, bf16[3,70,96]{1,0,2:T(4,128)(2,1)S(1)}, u32[]{:S(2)}, u32[]{:S(2)}) collective-permute-start(bf16[3,70,96]{1,0,2:T(4,128)(2,1)S(1)} %get-tuple-element.85), channel_id=1, source_target_pairs={{0,64},{8,72},{16,80},{24,88},{32,96},{40,104},{48,112},{56,120},{... | collective-permute-start | bytes 120968 | tf_op jit(solution)/shard_map/ppermute | solution.py:12
  26.6 27.1 %collective-permute-start.3 = (bf16[3,70,96]{1,0,2:T(4,128)(2,1)S(1)}, bf16[3,70,96]{1,0,2:T(4,128)(2,1)S(1)}, u32[]{:S(2)}, u32[]{:S(2)}) collective-permute-start(bf16[3,70,96]{1,0,2:T(4,128)(2,1)S(1)} %get-tuple-element.86), channel_id=1, source_target_pairs={{64,0},{72,8},{80,16},{88,24},{96,32},{104,40},{112,48},{120,56},{... | collective-permute-start | bytes 120968 | tf_op jit(solution)/shard_map/ppermute | solution.py:12
  112.9 105.1 %reduce-scatter.7.cloned.1.call-start = ((), (), s32[]{:S(2)}) async-start(), calls=%async_computation.2 | async-start | bytes 442368
  116.2 587.6 %all-reduce.5.cloned.1.call-start = ((), (), s32[]{:S(2)}) async-start(), calls=%async_computation.4 | async-start | bytes 4718592 | tf_op jit(solution)/shard_map/psum | solution.py:101
  198.5 20.4 %collective-permute-start.4 = (bf16[4,3,96]{1,0,2:T(4,128)(2,1)S(1)}, bf16[4,3,96]{1,0,2:T(4,128)(2,1)S(1)}, u32[]{:S(2)}, u32[]{:S(2)}) collective-permute-start(bf16[4,3,96]{1,0,2:T(4,128)(2,1)S(1)} %get-tuple-element.83), channel_id=1, source_target_pairs={{0,8},{8,16},{16,24},{24,32},{32,40},{40,48},{48,56},{56,64},{64,7... | collective-permute-start | bytes 6920 | tf_op jit(solution)/shard_map/ppermute | solution.py:12
  216.0 6.3 collective-permute-start.5
  222.6 286.4 %copy-start.9 = (f32[96]{0:T(128)S(1)}, f32[96]{0:T(128)}, u32[]{:S(2)}) copy-start(f32[96]{0:T(128)} %copy-done.8) | copy-start | bytes 1156
  222.6 286.4 %copy-start.11 = (f32[96]{0:T(128)S(1)}, f32[96]{0:T(128)}, u32[]{:S(2)}) copy-start(f32[96]{0:T(128)} %copy-done.10) | copy-start | bytes 1156
  222.6 286.4 %copy-start.13 = (f32[96]{0:T(128)S(1)}, f32[96]{0:T(128)}, u32[]{:S(2)}) copy-start(f32[96]{0:T(128)} %copy-done.12) | copy-start | bytes 1156
  222.6 286.4 %copy-start.15 = (f32[96]{0:T(128)S(1)}, f32[96]{0:T(128)}, u32[]{:S(2)}) copy-start(f32[96]{0:T(128)} %copy-done.14) | copy-start | bytes 1156
  222.6 286.4 %copy-start.17 = (f32[96]{0:T(128)S(1)}, f32[96]{0:T(128)}, u32[]{:S(2)}) copy-start(f32[96]{0:T(128)} %copy-done.16) | copy-start | bytes 1156
  222.6 286.4 %copy-start.19 = (f32[96]{0:T(128)S(1)}, f32[96]{0:T(128)}, u32[]{:S(2)}) copy-start(f32[96]{0:T(128)} %copy-done.18) | copy-start | bytes 1156
  222.6 286.4 %copy-start.21 = (f32[96]{0:T(128)S(1)}, f32[96]{0:T(128)}, u32[]{:S(2)}) copy-start(f32[96]{0:T(128)} %copy-done.20) | copy-start | bytes 1156
  222.7 286.4 %copy-start.23 = (f32[96]{0:T(128)S(1)}, f32[96]{0:T(128)}, u32[]{:S(2)}) copy-start(f32[96]{0:T(128)} %copy-done.22) | copy-start | bytes 1156
  222.7 286.4 %copy-start.25 = (f32[96]{0:T(128)S(1)}, f32[96]{0:T(128)}, u32[]{:S(2)}) copy-start(f32[96]{0:T(128)} %copy-done.24) | copy-start | bytes 1156
  222.7 286.4 %copy-start.27 = (f32[96]{0:T(128)S(1)}, f32[96]{0:T(128)}, u32[]{:S(2)}) copy-start(f32[96]{0:T(128)} %copy-done.26) | copy-start | bytes 1156
  222.7 286.4 %copy-start.29 = (f32[96]{0:T(128)S(1)}, f32[96]{0:T(128)}, u32[]{:S(2)}) copy-start(f32[96]{0:T(128)} %copy-done.28) | copy-start | bytes 1156
  222.7 286.4 %copy-start.31 = (f32[96]{0:T(128)S(1)}, f32[96]{0:T(128)}, u32[]{:S(2)}) copy-start(f32[96]{0:T(128)} %copy-done.30) | copy-start | bytes 1156
  222.7 286.4 %copy-start.33 = (f32[96]{0:T(128)S(1)}, f32[96]{0:T(128)}, u32[]{:S(2)}) copy-start(f32[96]{0:T(128)} %copy-done.32) | copy-start | bytes 1156
  223.0 285.2 %collective-permute-start.6 = (bf16[3,70,96]{1,0,2:T(4,128)(2,1)S(1)}, bf16[3,70,96]{1,0,2:T(4,128)(2,1)S(1)}, u32[]{:S(2)}, u32[]{:S(2)}) collective-permute-start(bf16[3,70,96]{1,0,2:T(4,128)(2,1)S(1)} %get-tuple-element.81), channel_id=1, source_target_pairs={{0,64},{8,72},{16,80},{24,88},{32,96},{40,104},{48,112},{56,120},{... | collective-permute-start | bytes 120968 | tf_op jit(solution)/shard_map/ppermute | solution.py:12
  229.0 279.3 %collective-permute-start.7 = (bf16[3,70,96]{1,0,2:T(4,128)(2,1)S(1)}, bf16[3,70,96]{1,0,2:T(4,128)(2,1)S(1)}, u32[]{:S(2)}, u32[]{:S(2)}) collective-permute-start(bf16[3,70,96]{1,0,2:T(4,128)(2,1)S(1)} %get-tuple-element.82), channel_id=1, source_target_pairs={{64,0},{72,8},{80,16},{88,24},{96,32},{104,40},{112,48},{120,56},{... | collective-permute-start | bytes 120968 | tf_op jit(solution)/shard_map/ppermute | solution.py:12
  (71 other events, 8630.3 us)
Sparse Core Ops, SparseCore 0:
  113.0 57.8 reduce-scatter.8
  173.7 42.8 reduce-scatter.6
Sparse Core Ops, SparseCore 1:
  120.3 583.5 all-reduce.4
where the time goes:
time: 717 us; the launch traced here: 715 us
  blocking collectives  358 us (50%)
  waiting for transfers between devices  236 us (33%)
  other arithmetic  46.2 us (6%)
  starting transfers between devices  35.7 us (5%)
  between operations  17.1 us (2%)
  local copies, waits for them, and re-layouts  16.4 us (2%)
    psum x1, blocking collectives, shards(): lax.psum((grad_in, grad_out, grad_kernel), 'sp')  277 us
    psum x1, waiting for transfers between devices, shards(): lax.psum((grad_in, grad_out, grad_kernel), 'sp')  181 us
    unnamed x5, waiting for transfers between devices  51.7 us
    ppermute x8, starting transfers between devices, passed_along(): return lax.ppermute(block, axis, route)  35.6 us
    all_gather x1, blocking collectives, shards(): grad_all = lax.all_gather(grad_map, 'ch', axis=2, tiled=True)  25.2 us
    all_gather x1, blocking collectives, shards(): lax.all_gather(((conv_f - mean) * rstd).astype(jnp.bfloat16), 'ch', axis=...  24.4 us
    reduce_sum x3, other arithmetic, shards(): jnp.sum(d_conv_f * padded[row:row + rows, col:col + cols], axis=(0, 1))  18.2 us
    psum x1, blocking collectives, shards(): lax.psum((jnp.sum(conv_f, axis=-1, keepdims=True), jnp.sum(conv_f * conv_...  16.1 us
  transfers between devices with their start and end apart: 11, of which 3 were waited for; matrix products, arithmetic and copies ran while one was open for 6% of the time, Pallas kernels for 0%

commit v1 on v0

v1 whole, which is shorter than its diff:
```python
import jax
import jax.numpy as jnp
from jax import lax
from jax.experimental import pallas as pl
from jax.experimental.pallas import tpu as pltpu
from jax.sharding import PartitionSpec as P

GRID_W = 8
MESH = pl.DeviceIdType.MESH
DIRS = ((-1, 0), (1, 0), (0, -1), (0, 1), (-1, -1), (-1, 1), (1, -1), (1, 1))
LEFT = 8
F32 = jnp.float32
BF16 = jnp.bfloat16


def greet(peers):
    barrier = pltpu.get_barrier_semaphore()
    for peer in peers:
        pl.semaphore_signal(barrier, inc=1, device_id=peer, device_id_type=MESH)
    pl.semaphore_wait(barrier, len(peers))


def send(src, dst, send_sem, recv_sem, peer):
    copy = pltpu.make_async_remote_copy(
        src_ref=src,
        dst_ref=dst,
        send_sem=send_sem,
        recv_sem=recv_sem,
        device_id=peer,
        device_id_type=MESH,
    )
    copy.start()
    return copy


def call(body, name, cid, out_shape, scratch):
    def run(*args):
        return pl.pallas_call(
            body,
            out_shape=out_shape,
            in_specs=[pl.BlockSpec(memory_space=pltpu.VMEM)] * len(args),
            out_specs=tuple([pl.BlockSpec(memory_space=pltpu.VMEM)] * len(out_shape)),
            scratch_shapes=scratch,
            compiler_params=pltpu.CompilerParams(
                collective_id=cid, has_side_effects=True, vmem_limit_bytes=48 * 2**20
            ),
            name=name,
        )(*args)

    return run


def shape(dims, dtype):
    return jax.ShapeDtypeStruct(dims, dtype)


def cut(block, dr, dc):
    if dr:
        block = block[:3] if dr < 0 else block[-3:]
    if dc:
        block = block[:, :3] if dc < 0 else block[:, -3:]
    return block


def strips(block):
    return [cut(block, dr, dc) for dr, dc in DIRS]


def start_margins(srcs, lands, send_sem, recv_sem):
    b, ch = lax.axis_index("sp"), lax.axis_index("ch")
    row, col = b // GRID_W, b % GRID_W
    peers = []
    for dr, dc in DIRS:
        r = lax.rem(row + dr + GRID_W, GRID_W)
        c = lax.rem(col + dc + GRID_W, GRID_W)
        peers.append((r * GRID_W + c, ch))
    greet(peers)
    return [
        send(srcs[k], lands[k], send_sem.at[k], recv_sem.at[k], peers[k]) for k in range(8)
    ]


def fill_margins(pad, block, lands):
    b = lax.axis_index("sp")
    row, col = b // GRID_W, b % GRID_W
    rows, cols = block.shape[0], block.shape[1]
    pad[3 : 3 + rows, LEFT : LEFT + cols] = block[...].astype(F32)
    for k, (dr, dc) in enumerate(DIRS):
        keep = jnp.logical_and(
            jnp.logical_and(row - dr >= 0, row - dr < GRID_W),
            jnp.logical_and(col - dc >= 0, col - dc < GRID_W),
        )
        value = lands[k][...].astype(F32)
        value = value * jnp.where(keep, 1.0, 0.0).astype(F32)
        top = 3 if dr == 0 else (0 if dr > 0 else 3 + rows)
        left = LEFT if dc == 0 else (LEFT - 3 if dc > 0 else LEFT + cols)
        pad[top : top + value.shape[0], left : left + value.shape[1]] = value


def front_kernel(*refs):
    block, taps = refs[0], refs[1]
    srcs = refs[2:10]
    conv, pad = refs[10], refs[11]
    lands, send_sem, recv_sem = refs[12:20], refs[20], refs[21]
    rows, cols = block.shape[0], block.shape[1]
    copies = start_margins(srcs, lands, send_sem, recv_sem)
    pad[...] = jnp.zeros_like(pad)
    for copy in copies:
        copy.wait()
    fill_margins(pad, block, lands)
    for p in range(rows):
        total = jnp.zeros(block.shape[1:], F32)
        for i in range(7):
            for j in range(7):
                t = i * 7 + j
                start = LEFT - 3 + j
                total = total + taps[t : t + 1, :] * pad[p + i, start : start + cols, :]
        conv[p] = total.astype(BF16)


def back_kernel(*refs):
    block, taps, grad_map, pad_x = refs[0:4]
    srcs = refs[4:12]
    grad_image, grad_taps = refs[12], refs[13]
    lands, pad, send_sem, recv_sem = refs[14:22], refs[22], refs[23], refs[24]
    rows, cols = block.shape[0], block.shape[1]
    copies = start_margins(srcs, lands, send_sem, recv_sem)
    pad[...] = jnp.zeros_like(pad)
    grad_taps[...] = jnp.zeros_like(grad_taps)
    for i in range(7):
        for j in range(7):
            t = i * 7 + j
            start = LEFT - 3 + j
            total = jnp.zeros(block.shape[1:], F32)
            for p in range(rows):
                total = total + block[p].astype(F32) * pad_x[p + i, start : start + cols, :]
            grad_taps[t : t + 1, :] = jnp.sum(total, axis=0, keepdims=True)
    for copy in copies:
        copy.wait()
    fill_margins(pad, block, lands)
    for p in range(rows):
        total = grad_map[p].astype(F32)
        for i in range(7):
            for j in range(7):
                t = i * 7 + j
                start = LEFT + 3 - j
                total = total + taps[t : t + 1, :] * pad[p + 6 - i, start : start + cols, :]
        grad_image[p] = total.astype(BF16)


def ch_peers(n):
    b, me = lax.axis_index("sp"), lax.axis_index("ch")
    return me, [(b, lax.rem(me + d, n)) for d in range(1, n)]


def send_stats(stat, me, peers, first, second, send_sem, recv_sem):
    stat[me, 0:1, :] = first
    stat[me, 1:2, :] = second
    return [
        send(stat.at[me], stat.at[me], send_sem.at[d], recv_sem.at[d], peer)
        for d, peer in enumerate(peers)
    ]


def sum_stats(stat, copies):
    for copy in copies:
        copy.wait()
    total = stat[0]
    for k in range(1, stat.shape[0]):
        total = total + stat[k]
    return total[0:1], total[1:2]


def gather_kernel(
    conv, grad_map, normed_all, grad_all, hat, rstd, stat, ssem, rsem
):
    n, panel, _ = normed_all.shape
    me, peers = ch_peers(n)
    chans = n * panel
    stat[me] = jnp.zeros(stat.shape[1:], F32)
    greet(peers)
    value = conv[...].astype(F32)
    stats = send_stats(
        stat,
        me,
        peers,
        jnp.sum(value, axis=0, keepdims=True),
        jnp.sum(value * value, axis=0, keepdims=True),
        ssem.at[0],
        rsem.at[0],
    )
    grads = [
        send(grad_map, grad_all.at[me], ssem.at[1, d], rsem.at[1, d], peer)
        for d, peer in enumerate(peers)
    ]
    grad_all[me] = grad_map[...]
    first, second = sum_stats(stat, stats)
    mean = first / chans
    var = second / chans - mean * mean
    scale = lax.rsqrt(var + 1e-06)
    rstd[...] = scale
    local = (value - mean) * scale
    hat[...] = local
    normed_all[me] = local.astype(BF16)
    outs = [
        send(normed_all.at[me], normed_all.at[me], ssem.at[2, d], rsem.at[2, d], peer)
        for d, peer in enumerate(peers)
    ]
    for copy in grads + outs:
        copy.wait()


def scatter_kernel(
    part_out, part_norm, hat, rstd, image, output, d_conv, land, stat, ssem, rsem
):
    n, panel, _ = part_out.shape
    me, peers = ch_peers(n)
    chans = n * panel
    stat[me] = jnp.zeros(stat.shape[1:], F32)
    greet(peers)
    norms = [
        send(part_norm.at[peer[1]], land.at[0, d], ssem.at[0, d], rsem.at[0, d], peer)
        for d, peer in enumerate(peers)
    ]
    outs = [
        send(part_out.at[peer[1]], land.at[1, d], ssem.at[1, d], rsem.at[1, d], peer)
        for d, peer in enumerate(peers)
    ]
    d_norm = part_norm[me].astype(F32)
    for d, copy in enumerate(norms):
        copy.wait()
        d_norm = d_norm + land[0, d].astype(F32)
    local = hat[...]
    stats = send_stats(
        stat,
        me,
        peers,
        jnp.sum(d_norm, axis=0, keepdims=True),
        jnp.sum(d_norm * local, axis=0, keepdims=True),
        ssem.at[2],
        rsem.at[2],
    )
    branch = part_out[me].astype(F32)
    for d, copy in enumerate(outs):
        copy.wait()
        branch = branch + land[1, d].astype(F32)
    output[...] = (image[...].astype(F32) + branch).astype(BF16)
    first, second = sum_stats(stat, stats)
    d_conv[...] = (
        rstd[...] * (d_norm - first / chans - local * second / chans)
    ).astype(BF16)


def reduce_kernel(
    grads, taps, out, taps_out, land0, tland0, mine, tmine, land1, tland1, land2, tland2, ssem, rsem
):
    b, ch = lax.axis_index("sp"), lax.axis_index("ch")
    ny, nz = grads.shape[1], land2.shape[0]
    core, y, z = b % 2, (b // 2) % ny, b // (2 * ny)
    other = (b + 1 - 2 * core, ch)
    ys = [lax.rem(y + d, ny) for d in range(1, ny)]
    zs = [lax.rem(z + d, nz) for d in range(1, nz)]
    y_peers = [((z * ny + k) * 2 + core, ch) for k in ys]
    z_peers = [((k * ny + y) * 2 + core, ch) for k in zs]
    greet([other] + y_peers + z_peers)

    firsts = [
        send(grads.at[1 - core, k], land0.at[k], ssem.at[0, k], rsem.at[0, k], other)
        for k in range(ny)
    ]
    tfirst = send(taps, tland0, ssem.at[1, 0], rsem.at[1, 0], other)
    tfirst.wait()
    tmine[...] = taps[...] + tland0[...]
    for k in range(ny):
        firsts[k].wait()
        mine[k] = (grads[core, k].astype(F32) + land0[k].astype(F32)).astype(BF16)

    moves, tmoves = [], []
    for d in range(ny - 1):
        moves.append(
            send(mine.at[ys[d]], land1.at[d], ssem.at[2, d], rsem.at[2, d], y_peers[d])
        )
        tmoves.append(
            send(tmine.at[ys[d]], tland1.at[d], ssem.at[3, d], rsem.at[3, d], y_peers[d])
        )
    total, ttotal = mine[y].astype(F32), tmine[y]
    for d in range(ny - 1):
        moves[d].wait()
        tmoves[d].wait()
        total = total + land1[d].astype(F32)
        ttotal = ttotal + tland1[d]
    land2[z] = total.astype(BF16)
    tland2[z] = ttotal

    moves, tmoves = [], []
    for d in range(nz - 1):
        moves.append(send(land2.at[z], land2.at[z], ssem.at[4, d], rsem.at[4, d], z_peers[d]))
        tmoves.append(send(tland2.at[z], tland2.at[z], ssem.at[5, d], rsem.at[5, d], z_peers[d]))
    for copy in moves + tmoves:
        copy.wait()
    total, ttotal = land2[0].astype(F32), tland2[0]
    for k in range(1, nz):
        total = total + land2[k].astype(F32)
        ttotal = ttotal + tland2[k]
    out[core, y] = total.astype(BF16)
    taps_out[y] = ttotal

    moves, tmoves, pairs = [], [], []
    for d in range(ny - 1):
        moves.append(
            send(out.at[core, y], out.at[core, y], ssem.at[6, d], rsem.at[6, d], y_peers[d])
        )
        tmoves.append(
            send(taps_out.at[y], taps_out.at[y], ssem.at[7, d], rsem.at[7, d], y_peers[d])
        )
    pairs.append(send(out.at[core, y], out.at[core, y], ssem.at[8, 0], rsem.at[8, 0], other))
    for d in range(ny - 1):
        moves[d].wait()
        k = lax.rem(y - d - 1 + ny, ny)
        pairs.append(
            send(out.at[core, k], out.at[core, k], ssem.at[8, d + 1], rsem.at[8, d + 1], other)
        )
    for copy in tmoves + pairs:
        copy.wait()


def make_shards(ny, nz):
    def shards(image, cotangent, kernel, w_in, w_out):
        block, grad_map = image[0], cotangent[0]
        rows, cols, panel = block.shape
        pixels = rows * cols
        n = w_in.shape[0] // panel
        hidden = w_in.shape[1]
        chans = w_in.shape[0]
        taps = kernel.astype(F32).reshape(49, panel)
        lands = [pltpu.VMEM(s.shape, BF16) for s in strips(block)]
        sems = [pltpu.SemaphoreType.DMA((8,)), pltpu.SemaphoreType.DMA((8,))]
        padded = (rows + 6, cols + 2 * LEFT, panel)

        conv, pad_x = call(
            front_kernel,
            "front",
            1,
            (shape(block.shape, BF16), shape(padded, F32)),
            lands + sems,
        )(block, taps, *strips(block))

        conv_t = conv.reshape(pixels, panel).T
        grad_t = grad_map.reshape(pixels, panel).T
        image_t = block.reshape(pixels, panel).T
        all_dims = (n, panel, pixels)
        normed_t, gall_t, hat, rstd = call(
            gather_kernel,
            "gather",
            2,
            (
                shape(all_dims, BF16),
                shape(all_dims, BF16),
                shape((panel, pixels), F32),
                shape((1, pixels), F32),
            ),
            [
                pltpu.VMEM((n, 8, pixels), F32),
                pltpu.SemaphoreType.DMA((3, n - 1)),
                pltpu.SemaphoreType.DMA((3, n - 1)),
            ],
        )(conv_t, grad_t)
        normed_t = normed_t.reshape(chans, pixels)
        gall_t = gall_t.reshape(chans, pixels)

        def mm(a, b, dims):
            return lax.dot_general(a, b, (dims, ((), ())), preferred_element_type=F32)

        pre = mm(w_in, normed_t, ((0,), (0,)))
        half = 0.5 * (1.0 + jax.scipy.special.erf(pre / jnp.sqrt(2.0)))
        act = (pre * half).astype(BF16)
        slope = half + pre * jnp.exp(-0.5 * pre * pre) / jnp.sqrt(2.0 * jnp.pi)
        d_act = mm(w_out, gall_t, ((1,), (0,)))
        d_pre = (d_act * slope).astype(BF16)
        part_out = mm(w_out, act, ((0,), (0,))).astype(BF16)
        part_norm = mm(w_in, d_pre, ((1,), (0,))).astype(BF16)
        grad_in = mm(normed_t, d_pre, ((1,), (1,))).astype(BF16)
        grad_out_t = mm(gall_t, act, ((1,), (1,))).astype(BF16)

        out_t, d_conv_t = call(
            scatter_kernel,
            "scatter",
            3,
            (shape((panel, pixels), BF16), shape((panel, pixels), BF16)),
            [
                pltpu.VMEM((2, n - 1, panel, pixels), BF16),
                pltpu.VMEM((n, 8, pixels), F32),
                pltpu.SemaphoreType.DMA((3, n - 1)),
                pltpu.SemaphoreType.DMA((3, n - 1)),
            ],
        )(part_out.reshape(all_dims), part_norm.reshape(all_dims), hat, rstd, image_t)
        output = out_t.T.reshape(block.shape)
        d_conv = d_conv_t.T.reshape(block.shape)

        grad_image, grad_taps = call(
            back_kernel,
            "back",
            4,
            (shape(block.shape, BF16), shape((56, panel), F32)),
            lands + [pltpu.VMEM(padded, F32)] + sems,
        )(d_conv, taps, grad_map, pad_x, *strips(d_conv))

        flat = grad_taps[:49].reshape(-1)
        flat = jnp.pad(flat, (0, ny * 8 * 128 - flat.shape[0])).reshape(ny, 8, 128)
        piece = chans // ny
        grads = jnp.stack([grad_in, grad_out_t]).reshape(2, ny, piece, hidden)
        total, taps_total = call(
            reduce_kernel,
            "reduce",
            5,
            (shape(grads.shape, BF16), shape(flat.shape, F32)),
            [
                pltpu.VMEM((ny, piece, hidden), BF16),
                pltpu.VMEM(flat.shape, F32),
                pltpu.VMEM((ny, piece, hidden), BF16),
                pltpu.VMEM(flat.shape, F32),
                pltpu.VMEM((ny - 1, piece, hidden), BF16),
                pltpu.VMEM((ny - 1, 8, 128), F32),
                pltpu.VMEM((nz, piece, hidden), BF16),
                pltpu.VMEM((nz, 8, 128), F32),
                pltpu.SemaphoreType.DMA((9, ny)),
                pltpu.SemaphoreType.DMA((9, ny)),
            ],
        )(grads, flat)
        total = total.astype(F32).reshape(2, chans, hidden)
        grad_kernel = taps_total.reshape(-1)[: 49 * panel].reshape(7, 7, panel)
        return output[None], grad_image[None], total[0], total[1].T, grad_kernel

    return shards


def solution(mesh):
    ny = 8
    nz = mesh.shape["sp"] // (2 * ny)
    return jax.shard_map(
        make_shards(ny, nz),
        mesh=mesh,
        in_specs=(
            P("sp", None, None, "ch"),
            P("sp", None, None, "ch"),
            P(None, None, "ch"),
            P(None, "ch"),
            P("ch", None),
        ),
        out_specs=(
            P("sp", None, None, "ch"),
            P("sp", None, None, "ch"),
            P(None, "ch"),
            P("ch", None),
            P(None, None, "ch"),
        ),
        check_vma=False,
    )
```

time: 717 us -> 140 us (0.20)
  blocking collectives: 358 us -> 0 us
  waiting for transfers between devices: 236 us -> 0 us
  Pallas kernels: 0 us -> 123 us
  other arithmetic: 46.2 us -> 0.14 us
  starting transfers between devices: 35.7 us -> 0 us
  between operations: 17.1 us -> 0.85 us
    psum x3 -> x0, blocking collectives: 308 us -> none  [the longest x1 277 us: shards(): lax.psum((grad_in, grad_out, grad_kernel), 'sp')]
    psum x1 -> x0, waiting for transfers between devices: 181 us -> none  [shards(): lax.psum((grad_in, grad_out, grad_kernel), 'sp')]
    pallas_call x0 -> x5, Pallas kernels: none -> 123 us  [run(): pl.pallas_call(body, out_shape=out_shape, in_specs=[pl.BlockSpec(memory_s...]
    unnamed x5 -> x0, waiting for transfers between devices: 51.7 us -> none
    all_gather x2 -> x0, blocking collectives: 49.7 us -> none  [the longest x1 25.2 us: shards(): grad_all = lax.all_gather(grad_map, 'ch', axis=2, tiled=True)]
    ppermute x8 -> x0, starting transfers between devices: 35.6 us -> none  [passed_along(): return lax.ppermute(block, axis, route)]
    reduce_sum x5 -> x0, other arithmetic: 30.9 us -> none  [the longest x3 18.2 us: shards(): jnp.sum(d_conv_f * padded[row:row + rows, col:col + cols], axis=(0, 1))]
    unnamed x181 -> x11, local copies, waits for them, and re-layouts: 14.2 us -> 1.49 us
  transfers between devices with their start and end apart: 11 -> 0, of which waited for: 3 -> 0; matrix products, arithmetic and copies ran while one was open for 6% -> 0% of each run, Pallas kernels for 0% -> 0%
where the time goes in v1:
time: 140 us; the launch traced here: 139 us
  Pallas kernels  123 us (88%)
  local copies, waits for them, and re-layouts  10.9 us (8%)
  matrix products  4.18 us (3%)
    pallas_call x5, Pallas kernels, run(): pl.pallas_call(body, out_shape=out_shape, in_specs=[pl.BlockSpec(memory_s...  123 us
    dot_general x6, matrix products, mm(): return lax.dot_general(a, b, (dims, ((), ())), preferred_element_type=F32)  4.18 us

profile of v1, /device:TPU:1, one launch (start us, length us, event | category | flops | bytes accessed | tf_op | source)
XLA Modules:
  0.0 139.0 jit_solution(3264090422444167438)
XLA Ops:
  0.6 0.9 slice_bitcast_fusion
  1.6 0.7 fusion.10
  2.3 0.7 reshape.72.refs_1_
  3.0 0.8 copy-done.1
  3.8 22.9 %front.1 = (bf16[4,64,96]{2,1,0:T(8,128)(2,1)S(1)}, f32[10,80,96]{2,1,0:T(8,128)S(1)}) custom-call(bf16[4,64,96]{2,1,0:T(8,128)(2,1)S(1)} %bitcast.59, f32[49,96]{1,0:T(8,128)S(1)} %reshape.72.refs_1_, bf16[3,64,96]{2,1,0:T(8,128)(2,1)S(1)} %get-tuple-element.41.refs_2_, bf16[3,64,96]{2,1,0:T(8,128)(2,1)S(1)} %get-tuple-element.40.refs_3_, ...), custom_call_target="tpu_custom_call" | custom-call | tf_op jit(solution)/shard_map/front/pallas_call | solution.py:38
  26.9 0.9 copy.21
  27.8 15.6 %gather.1 = (bf16[8,96,256]{2,1,0:T(8,128)(2,1)S(1)}, bf16[8,96,256]{2,1,0:T(8,128)(2,1)S(1)}, f32[96,256]{1,0:T(8,128)S(1)}, f32[1,256]{1,0:T(1,128)S(1)}) custom-call(bf16[96,256]{1,0:T(8,128)(2,1)S(1)} %bitcast.76, bf16[96,256]{1,0:T(8,128)(2,1)S(1)} %bitcast.77), custom_call_target="tpu_custom_call" | custom-call | tf_op jit(solution)/shard_map/gather/pallas_call | solution.py:38
  43.5 0.4 multiply_convert_fusion
  43.9 0.4 fusion.3
  44.4 0.4 convolution_convert_fusion.1
  44.7 0.4 convolution_convert_fusion
  45.1 0.1 pad_maximum_fusion.grads
  45.2 0.4 fusion.1
  45.6 0.2 copy.23
  45.8 2.2 %fusion = bf16[768,256]{0,1:T(8,128)(2,1)} fusion(bf16[384,256]{0,1:T(8,128)(2,1)S(1)} %get-tuple-element.52, bf16[384,768]{1,0:T(8,128)(2,1)} %param.9), kind=kOutput, calls=%fused_computation.4 | convolution fusion | flops 151191552 | bytes 1179648 | tf_op jit(solution)/shard_map/dot_general | solution.py:372
  48.0 1.2 copy.22
  49.4 14.7 %scatter.1 = (bf16[96,256]{1,0:T(8,128)(2,1)S(1)}, bf16[96,256]{1,0:T(8,128)(2,1)S(1)}) custom-call(bf16[8,96,256]{2,1,0:T(8,128)(2,1)S(1)} %bitcast.57, bf16[8,96,256]{2,1,0:T(8,128)(2,1)S(1)} %bitcast.56, f32[96,256]{1,0:T(8,128)S(1)} %get-tuple-element.20.hat, f32[1,256]{1,0:T(1,128)S(1)} %get-tuple-element.21.rstd, bf16[96,256]{1,0:T(8,128)(2,1)S(1)} %bitcast.75), custom_call_target="tpu_custom_call" | custom-call | tf_op jit(solution)/shard_map/scatter/pallas_call | solution.py:38
  64.6 17.7 %back.1 = (bf16[4,64,96]{2,1,0:T(8,128)(2,1)S(1)}, f32[56,96]{1,0:T(8,128)S(1)}) custom-call(bf16[4,64,96]{2,1,0:T(8,128)(2,1)S(1)} %bitcast.68, f32[49,96]{1,0:T(8,128)S(1)} %reshape.72.refs_1_, bf16[4,64,96]{2,1,0:T(8,128)(2,1)S(1)} %bitcast.70, f32[10,80,96]{2,1,0:T(8,128)S(1)} %get-tuple-element.24.refs_3_, bf16[3,64,96]{2,1,0:T(8,128)(2,1)S(1)} %bitcast.74, ...), custom_call_target="tpu_custom_call" | custom-call | tf_op jit(solution)/shard_map/back/pallas_call | solution.py:38
  82.3 51.9 %reduce.1 = (bf16[2,8,96,384]{3,2,1,0:T(8,128)(2,1)S(1)}, f32[8,8,128]{2,1,0:T(8,128)S(1)}) custom-call(bf16[2,8,96,384]{3,2,1,0:T(8,128)(2,1)S(1)} %pad_maximum_fusion.grads, f32[8,8,128]{2,1,0:T(8,128)S(1)} %pad_bitcast_fusion.taps), custom_call_target="tpu_custom_call" | custom-call | tf_op jit(solution)/shard_map/reduce/pallas_call | solution.py:38
  134.3 1.3 fusion.8
  135.5 1.4 copy.29
  136.9 0.7 reshape.70
  137.6 0.7 copy.25
  138.3 0.6 copy.31
  (22 shorter events, 0.8 us)
Async XLA Ops:
  0.6 42.9 %copy-start = (bf16[768,384]{1,0:T(8,128)(2,1)S(1)}, bf16[768,384]{1,0:T(8,128)(2,1)}, u32[]{:S(2)}) copy-start(bf16[768,384]{1,0:T(8,128)(2,1)} %param.8) | copy-start | bytes 1769476
  3.0 0.8 copy-start.1
  3.8 40.1 %copy-start.4 = (bf16[384,768]{1,0:T(8,128)(2,1)S(1)}, bf16[384,768]{1,0:T(8,128)(2,1)}, u32[]{:S(2)}) copy-start(bf16[384,768]{1,0:T(8,128)(2,1)} %param.9) | copy-start | bytes 1769476
  45.8 3.4 %copy-start.2 = (bf16[1,4,64,96]{3,2,1,0:T(8,128)(2,1)S(1)}, bf16[1,4,64,96]{3,2,1,0:T(8,128)(2,1)}, u32[]{:S(2)}) copy-start(bf16[1,4,64,96]{3,2,1,0:T(8,128)(2,1)} %param.5) | copy-start | bytes 147460
  48.0 16.5 %copy-start.3 = (bf16[1,4,64,96]{3,2,1,0:T(8,128)(2,1)S(1)}, bf16[1,4,64,96]{3,2,1,0:T(8,128)(2,1)}, u32[]{:S(2)}) copy-start(bf16[1,4,64,96]{3,2,1,0:T(8,128)(2,1)} %param.6) | copy-start | bytes 147460

commit v2 on v1

v2 whole, which is shorter than its diff:
```python
import jax
import jax.numpy as jnp
from jax import lax
from jax.experimental import pallas as pl
from jax.experimental.pallas import tpu as pltpu
from jax.sharding import PartitionSpec as P

GRID_W = 8
MESH = pl.DeviceIdType.MESH
DIRS = ((-1, 0), (1, 0), (0, -1), (0, 1), (-1, -1), (-1, 1), (1, -1), (1, 1))
EDGE = 16
LEFT = 8
F32 = jnp.float32
BF16 = jnp.bfloat16


def greet(peers):
    barrier = pltpu.get_barrier_semaphore()
    for peer in peers:
        pl.semaphore_signal(barrier, inc=1, device_id=peer, device_id_type=MESH)
    pl.semaphore_wait(barrier, len(peers))


def send(src, dst, send_sem, recv_sem, peer):
    copy = pltpu.make_async_remote_copy(
        src_ref=src,
        dst_ref=dst,
        send_sem=send_sem,
        recv_sem=recv_sem,
        device_id=peer,
        device_id_type=MESH,
    )
    copy.start()
    return copy


def call(body, name, cid, out_shape, scratch):
    def run(*args):
        return pl.pallas_call(
            body,
            out_shape=out_shape,
            in_specs=[pl.BlockSpec(memory_space=pltpu.VMEM)] * len(args),
            out_specs=tuple([pl.BlockSpec(memory_space=pltpu.VMEM)] * len(out_shape)),
            scratch_shapes=scratch,
            compiler_params=pltpu.CompilerParams(
                collective_id=cid, has_side_effects=True, vmem_limit_bytes=48 * 2**20
            ),
            name=name,
        )(*args)

    return run


def shape(dims, dtype):
    return jax.ShapeDtypeStruct(dims, dtype)


def window(dr, dc, rows, cols):
    r = slice(0, rows) if dr == 0 else (slice(0, 3) if dr < 0 else slice(rows - 3, rows))
    c = slice(0, cols) if dc == 0 else (slice(0, EDGE) if dc < 0 else slice(cols - EDGE, cols))
    return r, c


def margin_peers():
    b, ch = lax.axis_index("sp"), lax.axis_index("ch")
    row, col = b // GRID_W, b % GRID_W
    peers = []
    for dr, dc in DIRS:
        r = lax.rem(row + dr + GRID_W, GRID_W)
        c = lax.rem(col + dc + GRID_W, GRID_W)
        peers.append((r * GRID_W + c, ch))
    return peers


def start_margins(block, lands, send_sem, recv_sem, peers):
    rows, cols = block.shape[0], block.shape[1]
    copies = []
    for k, (dr, dc) in enumerate(DIRS):
        r, c = window(dr, dc, rows, cols)
        copies.append(
            send(block.at[r, c], lands[k], send_sem.at[k], recv_sem.at[k], peers[k])
        )
    return copies


def fill_margins(pad, block, lands):
    b = lax.axis_index("sp")
    row, col = b // GRID_W, b % GRID_W
    rows, cols = block.shape[0], block.shape[1]
    pad[3 : 3 + rows, LEFT : LEFT + cols] = block[...].astype(F32)
    for k, (dr, dc) in enumerate(DIRS):
        keep = jnp.logical_and(
            jnp.logical_and(row - dr >= 0, row - dr < GRID_W),
            jnp.logical_and(col - dc >= 0, col - dc < GRID_W),
        )
        value = lands[k][...].astype(F32)
        value = value * jnp.where(keep, 1.0, 0.0).astype(F32)
        if dc:
            value = value[:, :3] if dc < 0 else value[:, EDGE - 3 :]
        top = 3 if dr == 0 else (0 if dr > 0 else 3 + rows)
        left = LEFT if dc == 0 else (LEFT - 3 if dc > 0 else LEFT + cols)
        pad[top : top + value.shape[0], left : left + value.shape[1]] = value


def ch_peers(n):
    b, me = lax.axis_index("sp"), lax.axis_index("ch")
    return me, [(b, lax.rem(me + d, n)) for d in range(1, n)]


def send_stats(stat, me, peers, first, second, send_sem, recv_sem):
    stat[me, 0:1, :] = first
    stat[me, 1:2, :] = second
    return [
        send(stat.at[me], stat.at[me], send_sem.at[d], recv_sem.at[d], peer)
        for d, peer in enumerate(peers)
    ]


def sum_stats(stat, copies):
    for copy in copies:
        copy.wait()
    total = stat[0]
    for k in range(1, stat.shape[0]):
        total = total + stat[k]
    return total[0:1], total[1:2]


def to_channels(wide, panel):
    return wide[...].T[0:panel]


def to_pixels(tall, value, dims):
    rows, cols, panel = dims
    tall[0:panel, :] = value
    turned = tall[...].T
    return [turned[p * cols : (p + 1) * cols, 0:panel] for p in range(rows)]


def front_kernel(*refs):
    block, taps, grad_map = refs[0:3]
    normed_all, grad_all, hat, rstd, pad = refs[3:8]
    lands, msem, mrsem = refs[8:16], refs[16], refs[17]
    wide, stat, ssem, rsem = refs[18:22]
    rows, cols, panel = block.shape
    n = normed_all.shape[0]
    chans = n * panel
    me, peers = ch_peers(n)
    near = margin_peers()
    stat[me] = jnp.zeros(stat.shape[1:], F32)
    wide[...] = jnp.zeros_like(wide)
    for p in range(rows):
        wide[p * cols : (p + 1) * cols, 0:panel] = grad_map[p].astype(F32)
    grad_all[me] = to_channels(wide, panel).astype(BF16)
    greet(near + peers)
    copies = start_margins(block, lands, msem, mrsem, near)
    grads = [
        send(grad_all.at[me], grad_all.at[me], ssem.at[1, d], rsem.at[1, d], peer)
        for d, peer in enumerate(peers)
    ]
    pad[...] = jnp.zeros_like(pad)
    for copy in copies:
        copy.wait()
    fill_margins(pad, block, lands)
    for p in range(rows):
        total = jnp.zeros(block.shape[1:], F32)
        for i in range(7):
            for j in range(7):
                t = i * 7 + j
                start = LEFT - 3 + j
                total = total + taps[t : t + 1, :] * pad[p + i, start : start + cols, :]
        wide[p * cols : (p + 1) * cols, 0:panel] = total.astype(BF16).astype(F32)
    value = to_channels(wide, panel)
    stats = send_stats(
        stat,
        me,
        peers,
        jnp.sum(value, axis=0, keepdims=True),
        jnp.sum(value * value, axis=0, keepdims=True),
        ssem.at[0],
        rsem.at[0],
    )
    first, second = sum_stats(stat, stats)
    mean = first / chans
    var = second / chans - mean * mean
    scale = lax.rsqrt(var + 1e-06)
    rstd[...] = scale
    local = (value - mean) * scale
    hat[...] = local
    normed_all[me] = local.astype(BF16)
    outs = [
        send(normed_all.at[me], normed_all.at[me], ssem.at[2, d], rsem.at[2, d], peer)
        for d, peer in enumerate(peers)
    ]
    for copy in grads + outs:
        copy.wait()


def back_kernel(*refs):
    part_out, part_norm, hat, rstd, image, grad_map, taps, pad_x, grads = refs[0:9]
    output, grad_image, out, taps_out = refs[9:13]
    lands, msem, mrsem = refs[13:21], refs[21], refs[22]
    land, stat, csem, crsem, tall, d_conv, pad, mytaps = refs[23:31]
    land0, mine, land1, land2, tland0, tmine, tland1, tland2, ssem, rsem = refs[31:41]

    n, panel, pixels = part_out.shape
    rows, cols, _ = image.shape
    chans = n * panel
    b, ch = lax.axis_index("sp"), lax.axis_index("ch")
    me, peers = ch_peers(n)
    near = margin_peers()
    ny, nz = grads.shape[1], land2.shape[0]
    core, y, z = b % 2, (b // 2) % ny, b // (2 * ny)
    other = (b + 1 - 2 * core, ch)
    ys = [lax.rem(y + d, ny) for d in range(1, ny)]
    zs = [lax.rem(z + d, nz) for d in range(1, nz)]
    y_peers = [((z * ny + k) * 2 + core, ch) for k in ys]
    z_peers = [((k * ny + y) * 2 + core, ch) for k in zs]
    stat[me] = jnp.zeros(stat.shape[1:], F32)
    greet(peers + near + [other] + y_peers + z_peers)

    norms = [
        send(part_norm.at[peer[1]], land.at[0, d], csem.at[0, d], crsem.at[0, d], peer)
        for d, peer in enumerate(peers)
    ]
    outs = [
        send(part_out.at[peer[1]], land.at[1, d], csem.at[1, d], crsem.at[1, d], peer)
        for d, peer in enumerate(peers)
    ]
    order = ys + [y]
    firsts = [
        send(grads.at[1 - core, k], land0.at[k], ssem.at[0, d], rsem.at[0, d], other)
        for d, k in enumerate(order)
    ]
    tall[...] = jnp.zeros_like(tall)
    mytaps[...] = jnp.zeros_like(mytaps)
    pad[...] = jnp.zeros_like(pad)

    moves = []
    for d, k in enumerate(order):
        firsts[d].wait()
        mine[k] = (grads[core, k].astype(F32) + land0[k].astype(F32)).astype(BF16)
        if d < ny - 1:
            moves.append(
                send(mine.at[k], land1.at[d], ssem.at[2, d], rsem.at[2, d], y_peers[d])
            )

    d_norm = part_norm[me].astype(F32)
    for d, copy in enumerate(norms):
        copy.wait()
        d_norm = d_norm + land[0, d].astype(F32)
    local = hat[...]
    stats = send_stats(
        stat,
        me,
        peers,
        jnp.sum(d_norm, axis=0, keepdims=True),
        jnp.sum(d_norm * local, axis=0, keepdims=True),
        csem.at[2],
        crsem.at[2],
    )
    branch = part_out[me].astype(F32)
    for d, copy in enumerate(outs):
        copy.wait()
        branch = branch + land[1, d].astype(F32)
    for p, value in enumerate(to_pixels(tall, branch, image.shape)):
        output[p] = (image[p].astype(F32) + value).astype(BF16)
    first, second = sum_stats(stat, stats)
    back = rstd[...] * (d_norm - first / chans - local * second / chans)
    for p, value in enumerate(to_pixels(tall, back, image.shape)):
        d_conv[p] = value.astype(BF16)
    margins = start_margins(d_conv, lands, msem, mrsem, near)

    for i in range(7):
        for j in range(7):
            t = i * 7 + j
            start = LEFT - 3 + j
            total = jnp.zeros(image.shape[1:], F32)
            for p in range(rows):
                total = total + d_conv[p].astype(F32) * pad_x[p + i, start : start + cols, :]
            mytaps[t // 8, t % 8 : t % 8 + 1, 0:panel] = jnp.sum(total, axis=0, keepdims=True)
    tfirst = send(mytaps, tland0, ssem.at[1, 0], rsem.at[1, 0], other)

    total = mine[y].astype(F32)
    for d in range(ny - 1):
        moves[d].wait()
        total = total + land1[d].astype(F32)
    land2[z] = total.astype(BF16)
    moves = [
        send(land2.at[z], land2.at[z], ssem.at[4, d], rsem.at[4, d], z_peers[d])
        for d in range(nz - 1)
    ]

    tfirst.wait()
    tmine[...] = mytaps[...] + tland0[...]
    tmoves = [
        send(tmine.at[ys[d]], tland1.at[d], ssem.at[3, d], rsem.at[3, d], y_peers[d])
        for d in range(ny - 1)
    ]

    for copy in margins:
        copy.wait()
    fill_margins(pad, d_conv, lands)
    for p in range(rows):
        total = grad_map[p].astype(F32)
        for i in range(7):
            for j in range(7):
                t = i * 7 + j
                start = LEFT + 3 - j
                total = total + taps[t : t + 1, :] * pad[p + 6 - i, start : start + cols, :]
        grad_image[p] = total.astype(BF16)

    for copy in moves:
        copy.wait()
    total = land2[0].astype(F32)
    for k in range(1, nz):
        total = total + land2[k].astype(F32)
    out[core, y] = total.astype(BF16)
    moves = [
        send(out.at[core, y], out.at[core, y], ssem.at[6, d], rsem.at[6, d], y_peers[d])
        for d in range(ny - 1)
    ]
    pairs = [send(out.at[core, y], out.at[core, y], ssem.at[8, 0], rsem.at[8, 0], other)]

    ttotal = tmine[y]
    for d in range(ny - 1):
        tmoves[d].wait()
        ttotal = ttotal + tland1[d]
    tland2[z] = ttotal
    tmoves = [
        send(tland2.at[z], tland2.at[z], ssem.at[5, d], rsem.at[5, d], z_peers[d])
        for d in range(nz - 1)
    ]
    for copy in tmoves:
        copy.wait()
    ttotal = tland2[0]
    for k in range(1, nz):
        ttotal = ttotal + tland2[k]
    taps_out[y] = ttotal
    tmoves = [
        send(taps_out.at[y], taps_out.at[y], ssem.at[7, d], rsem.at[7, d], y_peers[d])
        for d in range(ny - 1)
    ]

    for d in range(ny - 1):
        moves[d].wait()
        k = lax.rem(y - d - 1 + ny, ny)
        pairs.append(
            send(out.at[core, k], out.at[core, k], ssem.at[8, d + 1], rsem.at[8, d + 1], other)
        )
    for copy in tmoves + pairs:
        copy.wait()


def make_shards(ny, nz):
    def shards(image, cotangent, kernel, w_in, w_out):
        block, grad_map = image[0], cotangent[0]
        rows, cols, panel = block.shape
        pixels = rows * cols
        n = w_in.shape[0] // panel
        hidden = w_in.shape[1]
        chans = w_in.shape[0]
        taps = kernel.astype(F32).reshape(49, panel)
        lands = []
        for dr, dc in DIRS:
            lands.append(
                pltpu.VMEM((3 if dr else rows, EDGE if dc else cols, panel), BF16)
            )

        def sems(*dims):
            return [pltpu.SemaphoreType.DMA(dims), pltpu.SemaphoreType.DMA(dims)]

        padded = (rows + 6, cols + 2 * LEFT, panel)
        all_dims = (n, panel, pixels)
        normed_t, gall_t, hat, rstd, pad_x = call(
            front_kernel,
            "front",
            1,
            (
                shape(all_dims, BF16),
                shape(all_dims, BF16),
                shape((panel, pixels), F32),
                shape((1, pixels), F32),
                shape(padded, F32),
            ),
            lands
            + sems(8)
            + [pltpu.VMEM((pixels, 128), F32), pltpu.VMEM((n, 8, pixels), F32)]
            + sems(3, n - 1),
        )(block, taps, grad_map)
        normed_t = normed_t.reshape(chans, pixels)
        gall_t = gall_t.reshape(chans, pixels)

        def mm(a, b, dims):
            return lax.dot_general(a, b, (dims, ((), ())), preferred_element_type=F32)

        pre = mm(w_in, normed_t, ((0,), (0,)))
        half = 0.5 * (1.0 + jax.scipy.special.erf(pre / jnp.sqrt(2.0)))
        act = (pre * half).astype(BF16)
        slope = half + pre * jnp.exp(-0.5 * pre * pre) / jnp.sqrt(2.0 * jnp.pi)
        d_act = mm(w_out, gall_t, ((1,), (0,)))
        d_pre = (d_act * slope).astype(BF16)
        part_out = mm(w_out, act, ((0,), (0,))).astype(BF16)
        part_norm = mm(w_in, d_pre, ((1,), (0,))).astype(BF16)
        grad_in = mm(normed_t, d_pre, ((1,), (1,))).astype(BF16)
        grad_out_t = mm(gall_t, act, ((1,), (1,))).astype(BF16)

        piece = chans // ny
        grads = jnp.stack([grad_in, grad_out_t]).reshape(2, ny, piece, hidden)
        tdims = (ny, 8, 128)
        output, grad_image, total, taps_total = call(
            back_kernel,
            "back",
            2,
            (
                shape(block.shape, BF16),
                shape(block.shape, BF16),
                shape(grads.shape, BF16),
                shape(tdims, F32),
            ),
            lands
            + sems(8)
            + [pltpu.VMEM((2, n - 1, panel, pixels), BF16), pltpu.VMEM((n, 8, pixels), F32)]
            + sems(3, n - 1)
            + [
                pltpu.VMEM((128, pixels), F32),
                pltpu.VMEM(block.shape, BF16),
                pltpu.VMEM(padded, F32),
                pltpu.VMEM(tdims, F32),
                pltpu.VMEM((ny, piece, hidden), BF16),
                pltpu.VMEM((ny, piece, hidden), BF16),
                pltpu.VMEM((ny - 1, piece, hidden), BF16),
                pltpu.VMEM((nz, piece, hidden), BF16),
                pltpu.VMEM(tdims, F32),
                pltpu.VMEM(tdims, F32),
                pltpu.VMEM((ny - 1, 8, 128), F32),
                pltpu.VMEM((nz, 8, 128), F32),
            ]
            + sems(9, ny),
        )(
            part_out.reshape(all_dims),
            part_norm.reshape(all_dims),
            hat,
            rstd,
            block,
            grad_map,
            taps,
            pad_x,
            grads,
        )
        total = total.astype(F32).reshape(2, chans, hidden)
        grad_kernel = taps_total.reshape(ny * 8, 128)[:49, :panel].reshape(7, 7, panel)
        return output[None], grad_image[None], total[0], total[1].T, grad_kernel

    return shards


def solution(mesh):
    ny = 8
    nz = mesh.shape["sp"] // (2 * ny)
    return jax.shard_map(
        make_shards(ny, nz),
        mesh=mesh,
        in_specs=(
            P("sp", None, None, "ch"),
            P("sp", None, None, "ch"),
            P(None, None, "ch"),
            P(None, "ch"),
            P("ch", None),
        ),
        out_specs=(
            P("sp", None, None, "ch"),
            P("sp", None, None, "ch"),
            P(None, "ch"),
            P("ch", None),
            P(None, None, "ch"),
        ),
        check_vma=False,
    )
```

time: 140 us -> 109 us (0.78)
  Pallas kernels: 123 us -> 92.8 us
  local copies, waits for them, and re-layouts: 10.9 us -> 13 us
  matrix products: 4.18 us -> 2.33 us
    pallas_call x5 -> x2, Pallas kernels: 123 us -> 92.8 us  [run(): pl.pallas_call(body, out_shape=out_shape, in_specs=[pl.BlockSpec(memory_s...]
    unnamed x11 -> x36, local copies, waits for them, and re-layouts: 1.49 us -> 7.88 us
    slice x10 -> x1, local copies, waits for them, and re-layouts: 1.96 us -> 0.01 us  [shards(): taps_total.reshape(ny * 8, 128)[:49, :panel].reshape(7, 7, panel)]
    dot_general x6, matrix products: 4.18 us -> 2.33 us  [mm(): return lax.dot_general(a, b, (dims, ((), ())), preferred_element_type=F32)]
where the time goes in v2:
time: 109 us
  Pallas kernels  92.8 us (85%)
  local copies, waits for them, and re-layouts  13 us (12%)
  matrix products  2.33 us (2%)
    pallas_call x2, Pallas kernels, run(): pl.pallas_call(body, out_shape=out_shape, in_specs=[pl.BlockSpec(memory_s...  92.8 us
    unnamed x36, local copies, waits for them, and re-layouts  7.88 us
    dot_general x6, matrix products, mm(): return lax.dot_general(a, b, (dims, ((), ())), preferred_element_type=F32)  2.33 us

profile of v2, /device:TPU:1, one launch (start us, length us, event | category | flops | bytes accessed | tf_op | source)
XLA Modules:
  0.0 109.1 jit_solution(4691855080014685124)
XLA Ops:
  0.6 0.8 reshape.52.refs_1_.refs_6_
  1.4 0.8 copy-done.4
  2.3 0.8 copy-done.6
  3.1 35.2 %front.1 = (bf16[8,96,256]{2,1,0:T(8,128)(2,1)S(1)}, bf16[8,96,256]{2,1,0:T(8,128)(2,1)S(1)}, f32[96,256]{1,0:T(8,128)S(1)}, f32[1,256]{1,0:T(1,128)S(1)}, f32[10,80,96]{2,1,0:T(8,128)S(1)}) custom-call(bf16[4,64,96]{2,1,0:T(8,128)(2,1)S(1)} %bitcast.44, f32[49,96]{1,0:T(8,128)S(1)} %reshape.52.refs_1_.refs_6_, bf16[4,64,96]{2,1,0:T(8,128)(2,1)S(1)} %bitcast.46), custom_call_target="tpu_custom_call" | custom-call | tf_op jit(solution)/shard_map/front/pallas_call | solution.py:39
  38.4 0.4 multiply_convert_fusion
  38.8 0.4 fusion.3
  39.3 0.4 convolution_convert_fusion
  39.6 0.4 fusion
  40.0 0.2 copy.10
  40.2 0.4 convolution_convert_fusion.1
  40.7 0.8 copy-done.15
  41.5 0.4 fusion.1
  41.9 0.9 copy.11
  42.8 1.0 copy-done.1
  43.8 1.0 copy-done.3
  44.8 0.9 copy-done.9
  45.7 57.6 %back.1 = (bf16[4,64,96]{2,1,0:T(8,128)(2,1)S(1)}, bf16[4,64,96]{2,1,0:T(8,128)(2,1)S(1)}, bf16[2,8,96,384]{3,2,1,0:T(8,128)(2,1)S(1)}, f32[8,8,128]{2,1,0:T(8,128)S(1)}) custom-call(bf16[8,96,256]{2,1,0:T(8,128)(2,1)S(1)} %bitcast.38, bf16[8,96,256]{2,1,0:T(8,128)(2,1)S(1)} %bitcast.39, f32[96,256]{1,0:T(8,128)S(1)} %copy-done.9, ...), custom_call_target="tpu_custom_call" | custom-call | tf_op jit(solution)/shard_map/back/pallas_call | solution.py:39
  103.4 0.6 copy-done.10
  104.0 0.6 copy-done.12
  104.6 0.6 reshape.50
  105.2 1.3 %fusion.8 = (f32[1,8,96,384]{3,2,1,0:T(8,128)S(1)}, f32[1,8,96,384]{3,2,1,0:T(8,128)}) fusion(bf16[2,8,96,384]{3,2,1,0:T(8,128)(2,1)S(1)} %get-tuple-element.21), kind=kLoop, calls=%fused_computation.18 | loop fusion | bytes 4718592 | tf_op jit(solution)/shard_map/slice | solution.py:452
  106.5 1.4 %copy.12 = f32[768,384]{0,1:T(8,128)} copy(f32[768,384]{1,0:T(8,128)S(1)} %bitcast.51) | data formatting | bytes 2359296 | tf_op jit(solution)/shard_map/squeeze | solution.py:452
  107.9 0.6 copy.15
  108.5 0.6 copy.16
  (28 shorter events, 0.2 us)
Async XLA Ops:
  0.6 37.7 %copy-start = (bf16[768,384]{1,0:T(8,128)(2,1)S(1)}, bf16[768,384]{1,0:T(8,128)(2,1)}, u32[]{:S(2)}) copy-start(bf16[768,384]{1,0:T(8,128)(2,1)} %param.8) | copy-start | bytes 1769476
  1.4 0.8 copy-start.4
  2.3 0.8 copy-start.6
  3.1 35.7 %copy-start.16 = (bf16[384,768]{1,0:T(8,128)(2,1)S(1)}, bf16[384,768]{1,0:T(8,128)(2,1)}, u32[]{:S(2)}) copy-start(bf16[384,768]{1,0:T(8,128)(2,1)} %param.9) | copy-start | bytes 1769476
  38.3 0.9 copy-start.2
  38.4 0.9 copy-start.8
  39.3 0.9 copy-start.14
  40.6 0.9 copy-start.15
  41.5 1.3 %copy-start.5 = (bf16[1,4,64,96]{3,2,1,0:T(8,128)(2,1)S(1)}, bf16[1,4,64,96]{3,2,1,0:T(8,128)(2,1)}, u32[]{:S(2)}) copy-start(bf16[1,4,64,96]{3,2,1,0:T(8,128)(2,1)} %param.5) | copy-start | bytes 147460
  41.5 1.3 %copy-start.7 = (bf16[1,4,64,96]{3,2,1,0:T(8,128)(2,1)S(1)}, bf16[1,4,64,96]{3,2,1,0:T(8,128)(2,1)}, u32[]{:S(2)}) copy-start(bf16[1,4,64,96]{3,2,1,0:T(8,128)(2,1)} %param.6) | copy-start | bytes 147460
  42.8 1.0 copy-start.1
  43.8 1.0 copy-start.3
  44.8 0.9 copy-start.9
  103.4 0.6 copy-start.10
  104.0 0.6 copy-start.12
  106.5 1.4 %copy-start.13 = (bf16[4,64,96]{2,1,0:T(8,128)(2,1)S(1)}, bf16[4,64,96]{2,1,0:T(8,128)(2,1)}, u32[]{:S(2)}) copy-start(bf16[4,64,96]{2,1,0:T(8,128)(2,1)} %copy-done.12) | copy-start | bytes 147460
  106.5 2.0 %copy-start.11 = (bf16[4,64,96]{2,1,0:T(8,128)(2,1)S(1)}, bf16[4,64,96]{2,1,0:T(8,128)(2,1)}, u32[]{:S(2)}) copy-start(bf16[4,64,96]{2,1,0:T(8,128)(2,1)} %copy-done.10) | copy-start | bytes 147460

commit v3 on v2

--- a/solution.py
+++ b/solution.py
@@ -10,6 +10,7 @@
 DIRS = ((-1, 0), (1, 0), (0, -1), (0, 1), (-1, -1), (-1, 1), (1, -1), (1, 1))
 EDGE = 16
 LEFT = 8
+CHUNKS = 3
 F32 = jnp.float32
 BF16 = jnp.bfloat16
 
@@ -43,7 +44,7 @@
             out_specs=tuple([pl.BlockSpec(memory_space=pltpu.VMEM)] * len(out_shape)),
             scratch_shapes=scratch,
             compiler_params=pltpu.CompilerParams(
-                collective_id=cid, has_side_effects=True, vmem_limit_bytes=48 * 2**20
+                collective_id=cid, has_side_effects=True, vmem_limit_bytes=20 * 2**20
             ),
             name=name,
         )(*args)
@@ -161,13 +162,13 @@
     for copy in copies:
         copy.wait()
     fill_margins(pad, block, lands)
+    rows_f = [taps[i].astype(F32) for i in range(7)]
     for p in range(rows):
         total = jnp.zeros(block.shape[1:], F32)
         for i in range(7):
             for j in range(7):
-                t = i * 7 + j
                 start = LEFT - 3 + j
-                total = total + taps[t : t + 1, :] * pad[p + i, start : start + cols, :]
+                total = total + rows_f[i][j : j + 1] * pad[p + i, start : start + cols, :]
         wide[p * cols : (p + 1) * cols, 0:panel] = total.astype(BF16).astype(F32)
     value = to_channels(wide, panel)
     stats = send_stats(
@@ -201,6 +202,7 @@
     lands, msem, mrsem = refs[13:21], refs[21], refs[22]
     land, stat, csem, crsem, tall, d_conv, pad, mytaps = refs[23:31]
     land0, mine, land1, land2, tland0, tmine, tland1, tland2, ssem, rsem = refs[31:41]
+    ring_send, ring_recv, pair_send, pair_recv = refs[41:45]
 
     n, panel, pixels = part_out.shape
     rows, cols, _ = image.shape
@@ -272,12 +274,11 @@
 
     for i in range(7):
         for j in range(7):
-            t = i * 7 + j
             start = LEFT - 3 + j
             total = jnp.zeros(image.shape[1:], F32)
             for p in range(rows):
                 total = total + d_conv[p].astype(F32) * pad_x[p + i, start : start + cols, :]
-            mytaps[t // 8, t % 8 : t % 8 + 1, 0:panel] = jnp.sum(total, axis=0, keepdims=True)
+            mytaps[i, j : j + 1, 0:panel] = jnp.sum(total, axis=0, keepdims=True)
     tfirst = send(mytaps, tland0, ssem.at[1, 0], rsem.at[1, 0], other)
 
     total = mine[y].astype(F32)
@@ -300,13 +301,13 @@
     for copy in margins:
         copy.wait()
     fill_margins(pad, d_conv, lands)
+    rows_f = [taps[i].astype(F32) for i in range(7)]
     for p in range(rows):
         total = grad_map[p].astype(F32)
         for i in range(7):
             for j in range(7):
-                t = i * 7 + j
                 start = LEFT + 3 - j
-                total = total + taps[t : t + 1, :] * pad[p + 6 - i, start : start + cols, :]
+                total = total + rows_f[i][j : j + 1] * pad[p + 6 - i, start : start + cols, :]
         grad_image[p] = total.astype(BF16)
 
     for copy in moves:
@@ -315,11 +316,26 @@
     for k in range(1, nz):
         total = total + land2[k].astype(F32)
     out[core, y] = total.astype(BF16)
-    moves = [
-        send(out.at[core, y], out.at[core, y], ssem.at[6, d], rsem.at[6, d], y_peers[d])
-        for d in range(ny - 1)
-    ]
-    pairs = [send(out.at[core, y], out.at[core, y], ssem.at[8, 0], rsem.at[8, 0], other)]
+    size = out.shape[2] // CHUNKS
+    ring = [((z * ny + k) * 2 + core, ch) for k in (lax.rem(y + 1, ny), lax.rem(y + ny - 1, ny))]
+
+    def part(k, c):
+        return out.at[core, k, c * size : (c + 1) * size]
+
+    def pass_on(way, step, c, k):
+        sems = ring_send.at[way, step, c], ring_recv.at[way, step, c]
+        return send(part(k, c), part(k, c), *sems, ring[way])
+
+    def share(step, c, k):
+        return send(part(k, c), part(k, c), pair_send.at[step, c], pair_recv.at[step, c], other)
+
+    def goes(way, step, c):
+        return step < ny // 2 - 1 or (step == ny // 2 - 1 and c % 2 == way)
+
+    flight = {
+        (way, 0, c): pass_on(way, 0, c, y) for c in range(CHUNKS) for way in range(2)
+    }
+    pairs = [share(0, c, y) for c in range(CHUNKS)]
 
     ttotal = tmine[y]
     for d in range(ny - 1):
@@ -341,12 +357,17 @@
         for d in range(ny - 1)
     ]
 
-    for d in range(ny - 1):
-        moves[d].wait()
-        k = lax.rem(y - d - 1 + ny, ny)
-        pairs.append(
-            send(out.at[core, k], out.at[core, k], ssem.at[8, d + 1], rsem.at[8, d + 1], other)
-        )
+    for step in range(ny // 2):
+        for c in range(CHUNKS):
+            for way in range(2):
+                if not goes(way, step, c):
+                    continue
+                flight[way, step, c].wait()
+                away = step + 1
+                k = lax.rem(y + (ny - away if way == 0 else away), ny)
+                if goes(way, away, c):
+                    flight[way, away, c] = pass_on(way, away, c, k)
+                pairs.append(share(away if way == 0 else ny - away, c, k))
     for copy in tmoves + pairs:
         copy.wait()
 
@@ -359,7 +380,6 @@
         n = w_in.shape[0] // panel
         hidden = w_in.shape[1]
         chans = w_in.shape[0]
-        taps = kernel.astype(F32).reshape(49, panel)
         lands = []
         for dr, dc in DIRS:
             lands.append(
@@ -386,7 +406,7 @@
             + sems(8)
             + [pltpu.VMEM((pixels, 128), F32), pltpu.VMEM((n, 8, pixels), F32)]
             + sems(3, n - 1),
-        )(block, taps, grad_map)
+        )(block, kernel, grad_map)
         normed_t = normed_t.reshape(chans, pixels)
         gall_t = gall_t.reshape(chans, pixels)
 
@@ -402,10 +422,15 @@
         part_out = mm(w_out, act, ((0,), (0,))).astype(BF16)
         part_norm = mm(w_in, d_pre, ((1,), (0,))).astype(BF16)
         grad_in = mm(normed_t, d_pre, ((1,), (1,))).astype(BF16)
-        grad_out_t = mm(gall_t, act, ((1,), (1,))).astype(BF16)
+        grad_out = mm(act, gall_t, ((1,), (1,))).astype(BF16)
 
         piece = chans // ny
-        grads = jnp.stack([grad_in, grad_out_t]).reshape(2, ny, piece, hidden)
+        grad_in = grad_in.reshape(ny, piece, hidden)
+        halves = [
+            grad_out[:, at : at + hidden].reshape(-1, piece, hidden)
+            for at in range(0, chans, hidden)
+        ]
+        grads = jnp.concatenate([grad_in] + halves).reshape(2, ny, piece, hidden)
         tdims = (ny, 8, 128)
         output, grad_image, total, taps_total = call(
             back_kernel,
@@ -435,7 +460,9 @@
                 pltpu.VMEM((ny - 1, 8, 128), F32),
                 pltpu.VMEM((nz, 8, 128), F32),
             ]
-            + sems(9, ny),
+            + sems(9, ny)
+            + sems(2, ny // 2, CHUNKS)
+            + sems(ny, CHUNKS),
         )(
             part_out.reshape(all_dims),
             part_norm.reshape(all_dims),
@@ -443,13 +470,18 @@
             rstd,
             block,
             grad_map,
-            taps,
+            kernel,
             pad_x,
             grads,
         )
-        total = total.astype(F32).reshape(2, chans, hidden)
-        grad_kernel = taps_total.reshape(ny * 8, 128)[:49, :panel].reshape(7, 7, panel)
-        return output[None], grad_image[None], total[0], total[1].T, grad_kernel
+        total = total.astype(F32)
+        grad_in = total[0].reshape(chans, hidden)
+        down = hidden // piece
+        grad_out = jnp.concatenate(
+            [total[1, k : k + down].reshape(hidden, hidden) for k in range(0, ny, down)], axis=1
+        )
+        grad_kernel = taps_total[:7, :7, :panel]
+        return output[None], grad_image[None], grad_in, grad_out, grad_kernel
 
     return shards
 

time: 109 us -> 109 us (level)
  local copies, waits for them, and re-layouts: 13 us -> 8.93 us
  Pallas kernels: 92.8 us -> 94.4 us
  other arithmetic: 0.14 us -> 1.26 us
    unnamed x36 -> x24, local copies, waits for them, and re-layouts: 7.88 us -> 5.04 us
    pallas_call x2, Pallas kernels: 92.8 us -> 94.4 us  [run(): pl.pallas_call(body, out_shape=out_shape, in_specs=[pl.BlockSpec(memory_s...]
    reshape x2 -> x0, local copies, waits for them, and re-layouts: 1.4 us -> none  [the longest x1 0.78 us: shards(): taps = kernel.astype(F32).reshape(49, panel)]
    squeeze x1 -> x0, local copies, waits for them, and re-layouts: 1.38 us -> none  [shards(): return (output[None], grad_image[None], total[0], total[1].T, grad_kernel)]
    slice x2 -> x4, local copies, waits for them, and re-layouts: 1.26 us -> 2.56 us  [the longest x1 1.09 us: shards(): grad_in = total[0].reshape(chans, hidden)]
    concatenate x0 -> x2, other arithmetic: none -> 1.26 us  [the longest x1 1.1 us: shards(): jnp.concatenate([total[1, k:k + down].reshape(hidden, hidden) for k in ra...]
where the time goes in v3:
time: 109 us
  Pallas kernels  94.4 us (87%)
  local copies, waits for them, and re-layouts  8.93 us (8%)
  matrix products  3.11 us (3%)
  other arithmetic  1.26 us (1%)
    pallas_call x2, Pallas kernels, run(): pl.pallas_call(body, out_shape=out_shape, in_specs=[pl.BlockSpec(memory_s...  94.4 us
    unnamed x24, local copies, waits for them, and re-layouts  5.04 us
    dot_general x6, matrix products, mm(): return lax.dot_general(a, b, (dims, ((), ())), preferred_element_type=F32)  3.11 us

profile of v3, /device:TPU:1, one launch (start us, length us, event | category | flops | bytes accessed | tf_op | source)
XLA Modules:
  0.0 108.5 jit_solution(309647581118372119)
XLA Ops:
  0.6 0.0 copy-start
  0.7 0.9 copy-done.1
  1.6 0.8 copy-done.3
  2.4 0.7 copy-done.5
  3.1 35.2 %front.1 = (bf16[8,96,256]{2,1,0:T(8,128)(2,1)S(1)}, bf16[8,96,256]{2,1,0:T(8,128)(2,1)S(1)}, f32[96,256]{1,0:T(8,128)S(1)}, f32[1,256]{1,0:T(1,128)S(1)}, f32[10,80,96]{2,1,0:T(8,128)S(1)}) custom-call(bf16[4,64,96]{2,1,0:T(8,128)(2,1)S(1)} %bitcast.46, bf16[7,7,96]{2,1,0:T(8,128)(2,1)S(1)} %copy-done.5, bf16[4,64,96]{2,1,0:T(8,128)(2,1)S(1)} %bitcast.48), custom_call_target="tpu_custom_call" | custom-call | tf_op jit(solution)/shard_map/front/pallas_call | solution.py:40
  38.4 0.4 multiply_convert_fusion
  38.8 0.4 fusion.3
  39.2 0.4 convolution_convert_fusion
  39.6 0.8 fusion.9
  40.4 0.4 fusion
  40.8 0.2 copy.10
  41.0 0.4 convolution_convert_fusion.1
  41.3 0.6 copy-done.7
  41.9 0.2 pad_maximum_fusion
  42.1 0.7 copy-done.9
  42.8 1.1 %fusion.1 = bf16[768,256]{0,1:T(8,128)(2,1)} fusion(bf16[384,256]{0,1:T(8,128)(2,1)S(1)} %copy-done.9, bf16[768,384]{1,0:T(8,128)(2,1)S(1)} %copy-done), kind=kOutput, calls=%fused_computation.5 | convolution fusion | flops 151191552 | bytes 1179648 | tf_op jit(solution)/shard_map/dot_general | solution.py:414
  44.0 1.2 %copy.11 = bf16[768,256]{1,0:T(8,128)(2,1)S(1)} copy(bf16[768,256]{0,1:T(8,128)(2,1)} %fusion.1) | data formatting | bytes 786432 | tf_op jit(solution)/shard_map/convert_element_type | solution.py:423
  45.2 59.2 %back.1 = (bf16[4,64,96]{2,1,0:T(8,128)(2,1)S(1)}, bf16[4,64,96]{2,1,0:T(8,128)(2,1)S(1)}, bf16[2,8,96,384]{3,2,1,0:T(8,128)(2,1)S(1)}, f32[8,8,128]{2,1,0:T(8,128)S(1)}) custom-call(bf16[8,96,256]{2,1,0:T(8,128)(2,1)S(1)} %bitcast.40, bf16[8,96,256]{2,1,0:T(8,128)(2,1)S(1)} %bitcast.41, f32[96,256]{1,0:T(8,128)S(1)} %get-tuple-element.16.refs_2_, ...), custom_call_target="tpu_custom_call" | custom-call | tf_op jit(solution)/shard_map/back/pallas_call | solution.py:40
  104.4 0.6 slice.23
  105.0 1.1 %slice.26 = f32[1,8,96,384]{3,2,1,0:T(8,128)} slice(bf16[2,8,96,384]{3,2,1,0:T(8,128)(2,1)S(1)} %get-tuple-element.21), slice={[0:1], [0:8], [0:96], [0:384]} | slice | bytes 2359296 | tf_op jit(solution)/shard_map/slice | solution.py:478
  106.1 0.1 fusion.8
  106.2 1.1 %pad_maximum_fusion.1 = f32[384,768]{1,0:T(8,128)} fusion(f32[384,384]{1,0:T(8,128)S(1)} %bitcast.54, f32[384,384]{1,0:T(8,128)S(1)} %bitcast.53), kind=kLoop, calls=%fused_computation.10 | loop fusion | flops 294912 | bytes 2359296 | tf_op jit(solution)/shard_map/concatenate | solution.py:480
  107.3 0.6 copy.14
  107.9 0.6 copy.15
  (16 shorter events, 0.0 us)
Async XLA Ops:
  0.6 37.7 %copy-start = (bf16[768,384]{1,0:T(8,128)(2,1)S(1)}, bf16[768,384]{1,0:T(8,128)(2,1)}, u32[]{:S(2)}) copy-start(bf16[768,384]{1,0:T(8,128)(2,1)} %param.8) | copy-start | bytes 1769476
  0.6 0.9 copy-start.1
  1.6 0.8 copy-start.3
  2.4 0.7 copy-start.5
  3.1 35.7 %copy-start.10 = (bf16[384,768]{1,0:T(8,128)(2,1)S(1)}, bf16[384,768]{1,0:T(8,128)(2,1)}, u32[]{:S(2)}) copy-start(bf16[384,768]{1,0:T(8,128)(2,1)} %param.9) | copy-start | bytes 1769476
  39.2 1.7 %copy-start.8 = (bf16[384,256]{0,1:T(8,128)(2,1)}, bf16[384,256]{0,1:T(8,128)(2,1)S(1)}, u32[]{:S(2)}) copy-start(bf16[384,256]{0,1:T(8,128)(2,1)S(1)} %fusion.3) | copy-start | bytes 589828
  40.9 1.0 copy-start.7
  41.9 0.9 copy-start.9
  42.1 3.1 %copy-start.2 = (bf16[1,4,64,96]{3,2,1,0:T(8,128)(2,1)S(1)}, bf16[1,4,64,96]{3,2,1,0:T(8,128)(2,1)}, u32[]{:S(2)}) copy-start(bf16[1,4,64,96]{3,2,1,0:T(8,128)(2,1)} %param.5) | copy-start | bytes 147460
  42.1 3.1 %copy-start.4 = (bf16[1,4,64,96]{3,2,1,0:T(8,128)(2,1)S(1)}, bf16[1,4,64,96]{3,2,1,0:T(8,128)(2,1)}, u32[]{:S(2)}) copy-start(bf16[1,4,64,96]{3,2,1,0:T(8,128)(2,1)} %param.6) | copy-start | bytes 147460
  42.1 3.1 %copy-start.6 = (bf16[7,7,96]{2,1,0:T(8,128)(2,1)S(1)}, bf16[7,7,96]{2,1,0:T(8,128)(2,1)}, u32[]{:S(2)}) copy-start(bf16[7,7,96]{2,1,0:T(8,128)(2,1)} %refs_6_.1) | copy-start | bytes 28228

commit v4 on v3

--- a/solution.py
+++ b/solution.py
@@ -203,6 +203,7 @@
     land, stat, csem, crsem, tall, d_conv, pad, mytaps = refs[23:31]
     land0, mine, land1, land2, tland0, tmine, tland1, tland2, ssem, rsem = refs[31:41]
     ring_send, ring_recv, pair_send, pair_recv = refs[41:45]
+    sum_send, sum_recv, across_send, across_recv = refs[45:49]
 
     n, panel, pixels = part_out.shape
     rows, cols, _ = image.shape
@@ -228,7 +229,9 @@
         send(part_out.at[peer[1]], land.at[1, d], csem.at[1, d], crsem.at[1, d], peer)
         for d, peer in enumerate(peers)
     ]
-    order = ys + [y]
+    half = ny // 2
+    away = [half] + [a for d in range(half - 1, 0, -1) for a in (d, ny - d)] + [0]
+    order = [lax.rem(y + a, ny) for a in away]
     firsts = [
         send(grads.at[1 - core, k], land0.at[k], ssem.at[0, d], rsem.at[0, d], other)
         for d, k in enumerate(order)
@@ -237,14 +240,53 @@
     mytaps[...] = jnp.zeros_like(mytaps)
     pad[...] = jnp.zeros_like(pad)
 
-    moves = []
+    size = out.shape[2] // CHUNKS
+    ring = [((z * ny + k) * 2 + core, ch) for k in (lax.rem(y + 1, ny), lax.rem(y + ny - 1, ny))]
     for d, k in enumerate(order):
         firsts[d].wait()
         mine[k] = (grads[core, k].astype(F32) + land0[k].astype(F32)).astype(BF16)
-        if d < ny - 1:
-            moves.append(
-                send(mine.at[k], land1.at[d], ssem.at[2, d], rsem.at[2, d], y_peers[d])
-            )
+    sums, moves = {}, []
+    for step in range(half + 1):
+        for c in range(CHUNKS):
+            part_rows = slice(c * size, (c + 1) * size)
+            for way in range(2):
+                reach = half if c % 2 == way else half - 1
+                left = reach - step
+                if left < 0:
+                    continue
+                k = lax.rem(y + (left if way == 0 else ny - left), ny)
+                src = mine.at[k, part_rows]
+                if step:
+                    sums[way, step - 1, c].wait()
+                    src = land1.at[way, step - 1, part_rows]
+                if left and step:
+                    src[...] = (src[...].astype(F32) + mine[k, part_rows].astype(F32)).astype(BF16)
+                if left:
+                    sums[way, step, c] = send(
+                        src,
+                        land1.at[way, step, part_rows],
+                        sum_send.at[way, step, c],
+                        sum_recv.at[way, step, c],
+                        ring[way],
+                    )
+            if step == half:
+                total = mine[y, part_rows].astype(F32)
+                for way in range(2):
+                    last = (half if c % 2 == way else half - 1) - 1
+                    total = total + land1[way, last, part_rows].astype(F32)
+                land2[z, part_rows] = total.astype(BF16)
+                moves.append(
+                    [
+                        send(
+                            land2.at[z, part_rows],
+                            land2.at[z, part_rows],
+                            across_send.at[c, d],
+                            across_recv.at[c, d],
+                            z_peers[d],
+                        )
+                        for d in range(nz - 1)
+                    ]
+                )
 
     d_norm = part_norm[me].astype(F32)
     for d, copy in enumerate(norms):
@@ -281,79 +323,36 @@
             mytaps[i, j : j + 1, 0:panel] = jnp.sum(total, axis=0, keepdims=True)
     tfirst = send(mytaps, tland0, ssem.at[1, 0], rsem.at[1, 0], other)
 
-    total = mine[y].astype(F32)
-    for d in range(ny - 1):
-        moves[d].wait()
-        total = total + land1[d].astype(F32)
-    land2[z] = total.astype(BF16)
-    moves = [
-        send(land2.at[z], land2.at[z], ssem.at[4, d], rsem.at[4, d], z_peers[d])
-        for d in range(nz - 1)
-    ]
+    def part(k, c):
+        return out.at[core, k, c * size : (c + 1) * size]
+
+    def pass_on(way, step, c, k):
+        sems = ring_send.at[way, step, c], ring_recv.at[way, step, c]
+        return send(part(k, c), part(k, c), *sems, ring[way])
+
+    def share(step, c, k):
+        return send(part(k, c), part(k, c), pair_send.at[step, c], pair_recv.at[step, c], other)
+
+    def goes(way, step, c):
+        return step < ny // 2 - 1 or (step == ny // 2 - 1 and c % 2 == way)
+
+    flight, pairs = {}, []
+    for c in range(CHUNKS):
+        part_rows = slice(c * size, (c + 1) * size)
+        for copy in moves[c]:
+            copy.wait()
+        total = land2[0, part_rows].astype(F32)
+        for k in range(1, nz):
+            total = total + land2[k, part_rows].astype(F32)
+        out[core, y, part_rows] = total.astype(BF16)
+        for way in range(2):
+            flight[way, 0, c] = pass_on(way, 0, c, y)
+        pairs.append(share(0, c, y))
 
     tfirst.wait()
     tmine[...] = mytaps[...] + tland0[...]
     tmoves = [
         send(tmine.at[ys[d]], tland1.at[d], ssem.at[3, d], rsem.at[3, d], y_peers[d])
-        for d in range(ny - 1)
-    ]
-
-    for copy in margins:
-        copy.wait()
-    fill_margins(pad, d_conv, lands)
-    rows_f = [taps[i].astype(F32) for i in range(7)]
-    for p in range(rows):
-        total = grad_map[p].astype(F32)
-        for i in range(7):
-            for j in range(7):
-                start = LEFT + 3 - j
-                total = total + rows_f[i][j : j + 1] * pad[p + 6 - i, start : start + cols, :]
-        grad_image[p] = total.astype(BF16)
-
-    for copy in moves:
-        copy.wait()
-    total = land2[0].astype(F32)
-    for k in range(1, nz):
-        total = total + land2[k].astype(F32)
-    out[core, y] = total.astype(BF16)
-    size = out.shape[2] // CHUNKS
-    ring = [((z * ny + k) * 2 + core, ch) for k in (lax.rem(y + 1, ny), lax.rem(y + ny - 1, ny))]
-
-    def part(k, c):
-        return out.at[core, k, c * size : (c + 1) * size]
-
-    def pass_on(way, step, c, k):
-        sems = ring_send.at[way, step, c], ring_recv.at[way, step, c]
-        return send(part(k, c), part(k, c), *sems, ring[way])
-
-    def share(step, c, k):
-        return send(part(k, c), part(k, c), pair_send.at[step, c], pair_recv.at[step, c], other)
-
-    def goes(way, step, c):
-        return step < ny // 2 - 1 or (step == ny // 2 - 1 and c % 2 == way)
-
-    flight = {
-        (way, 0, c): pass_on(way, 0, c, y) for c in range(CHUNKS) for way in range(2)
-    }
-    pairs = [share(0, c, y) for c in range(CHUNKS)]
-
-    ttotal = tmine[y]
-    for d in range(ny - 1):
-        tmoves[d].wait()
-        ttotal = ttotal + tland1[d]
-    tland2[z] = ttotal
-    tmoves = [
-        send(tland2.at[z], tland2.at[z], ssem.at[5, d], rsem.at[5, d], z_peers[d])
-        for d in range(nz - 1)
-    ]
-    for copy in tmoves:
-        copy.wait()
-    ttotal = tland2[0]
-    for k in range(1, nz):
-        ttotal = ttotal + tland2[k]
-    taps_out[y] = ttotal
-    tmoves = [
-        send(taps_out.at[y], taps_out.at[y], ssem.at[7, d], rsem.at[7, d], y_peers[d])
         for d in range(ny - 1)
     ]
 
@@ -368,6 +367,39 @@
                 if goes(way, away, c):
                     flight[way, away, c] = pass_on(way, away, c, k)
                 pairs.append(share(away if way == 0 else ny - away, c, k))
+        if step == 0:
+            ttotal = tmine[y]
+            for d in range(ny - 1):
+                tmoves[d].wait()
+                ttotal = ttotal + tland1[d]
+            tland2[z] = ttotal
+            tmoves = [
+                send(tland2.at[z], tland2.at[z], ssem.at[5, d], rsem.at[5, d], z_peers[d])
+                for d in range(nz - 1)
+            ]
+        if step == 2:
+            for copy in tmoves:
+                copy.wait()
+            ttotal = tland2[0]
+            for k in range(1, nz):
+                ttotal = ttotal + tland2[k]
+            taps_out[y] = ttotal
+            tmoves = [
+                send(taps_out.at[y], taps_out.at[y], ssem.at[7, d], rsem.at[7, d], y_peers[d])
+                for d in range(ny - 1)
+            ]
+    for copy in margins:
+        copy.wait()
+    fill_margins(pad, d_conv, lands)
+    rows_f = [taps[i].astype(F32) for i in range(7)]
+    for p in range(rows):
+        total = grad_map[p].astype(F32)
+        for i in range(7):
+            for j in range(7):
+                start = LEFT + 3 - j
+                total = total + rows_f[i][j : j + 1] * pad[p + 6 - i, start : start + cols, :]
+        grad_image[p] = total.astype(BF16)
+
     for copy in tmoves + pairs:
         copy.wait()
 
@@ -453,7 +485,7 @@
                 pltpu.VMEM(tdims, F32),
                 pltpu.VMEM((ny, piece, hidden), BF16),
                 pltpu.VMEM((ny, piece, hidden), BF16),
-                pltpu.VMEM((ny - 1, piece, hidden), BF16),
+                pltpu.VMEM((2, ny // 2, piece, hidden), BF16),
                 pltpu.VMEM((nz, piece, hidden), BF16),
                 pltpu.VMEM(tdims, F32),
                 pltpu.VMEM(tdims, F32),
@@ -462,7 +494,9 @@
             ]
             + sems(9, ny)
             + sems(2, ny // 2, CHUNKS)
-            + sems(ny, CHUNKS),
+            + sems(ny, CHUNKS)
+            + sems(2, ny // 2, CHUNKS)
+            + sems(CHUNKS, nz - 1),
         )(
             part_out.reshape(all_dims),
             part_norm.reshape(all_dims),

time: 109 us -> 104 us (0.954)
  Pallas kernels: 94.4 us -> 89.3 us
    pallas_call x2, Pallas kernels: 94.4 us -> 89.3 us  [run(): pl.pallas_call(body, out_shape=out_shape, in_specs=[pl.BlockSpec(memory_s...]
where the time goes in v4:
time: 104 us; the launch traced here: 103 us
  Pallas kernels  89.3 us (86%)
  local copies, waits for them, and re-layouts  8.93 us (9%)
  matrix products  3.11 us (3%)
  other arithmetic  1.26 us (1%)
    pallas_call x2, Pallas kernels, run(): pl.pallas_call(body, out_shape=out_shape, in_specs=[pl.BlockSpec(memory_s...  89.3 us
    unnamed x24, local copies, waits for them, and re-layouts  5.04 us
    dot_general x6, matrix products, mm(): return lax.dot_general(a, b, (dims, ((), ())), preferred_element_type=F32)  3.11 us

profile of v4, /device:TPU:1, one launch (start us, length us, event | category | flops | bytes accessed | tf_op | source)
XLA Modules:
  0.0 103.4 jit_solution(2670614344428807124)
XLA Ops:
  0.6 0.0 copy-start
  0.7 0.9 copy-done.1
  1.6 0.8 copy-done.3
  2.4 0.7 copy-done.5
  3.1 35.2 %front.1 = (bf16[8,96,256]{2,1,0:T(8,128)(2,1)S(1)}, bf16[8,96,256]{2,1,0:T(8,128)(2,1)S(1)}, f32[96,256]{1,0:T(8,128)S(1)}, f32[1,256]{1,0:T(1,128)S(1)}, f32[10,80,96]{2,1,0:T(8,128)S(1)}) custom-call(bf16[4,64,96]{2,1,0:T(8,128)(2,1)S(1)} %bitcast.46, bf16[7,7,96]{2,1,0:T(8,128)(2,1)S(1)} %copy-done.5, bf16[4,64,96]{2,1,0:T(8,128)(2,1)S(1)} %bitcast.48), custom_call_target="tpu_custom_call" | custom-call | tf_op jit(solution)/shard_map/front/pallas_call | solution.py:40
  38.4 0.4 multiply_convert_fusion
  38.8 0.4 fusion.3
  39.2 0.4 convolution_convert_fusion
  39.6 0.8 fusion.9
  40.4 0.4 fusion
  40.8 0.2 copy.10
  41.0 0.4 convolution_convert_fusion.1
  41.3 0.6 copy-done.7
  41.9 0.2 pad_maximum_fusion
  42.1 0.7 copy-done.9
  42.8 1.1 %fusion.1 = bf16[768,256]{0,1:T(8,128)(2,1)} fusion(bf16[384,256]{0,1:T(8,128)(2,1)S(1)} %copy-done.9, bf16[768,384]{1,0:T(8,128)(2,1)S(1)} %copy-done), kind=kOutput, calls=%fused_computation.5 | convolution fusion | flops 151191552 | bytes 1179648 | tf_op jit(solution)/shard_map/dot_general | solution.py:446
  44.0 1.2 %copy.11 = bf16[768,256]{1,0:T(8,128)(2,1)S(1)} copy(bf16[768,256]{0,1:T(8,128)(2,1)} %fusion.1) | data formatting | bytes 786432 | tf_op jit(solution)/shard_map/convert_element_type | solution.py:455
  45.2 54.1 %back.1 = (bf16[4,64,96]{2,1,0:T(8,128)(2,1)S(1)}, bf16[4,64,96]{2,1,0:T(8,128)(2,1)S(1)}, bf16[2,8,96,384]{3,2,1,0:T(8,128)(2,1)S(1)}, f32[8,8,128]{2,1,0:T(8,128)S(1)}) custom-call(bf16[8,96,256]{2,1,0:T(8,128)(2,1)S(1)} %bitcast.40, bf16[8,96,256]{2,1,0:T(8,128)(2,1)S(1)} %bitcast.41, f32[96,256]{1,0:T(8,128)S(1)} %get-tuple-element.16.refs_2_, ...), custom_call_target="tpu_custom_call" | custom-call | tf_op jit(solution)/shard_map/back/pallas_call | solution.py:40
  99.2 0.6 slice.23
  99.9 1.1 %slice.26 = f32[1,8,96,384]{3,2,1,0:T(8,128)} slice(bf16[2,8,96,384]{3,2,1,0:T(8,128)(2,1)S(1)} %get-tuple-element.21), slice={[0:1], [0:8], [0:96], [0:384]} | slice | bytes 2359296 | tf_op jit(solution)/shard_map/slice | solution.py:512
  101.0 0.1 fusion.8
  101.0 1.1 %pad_maximum_fusion.1 = f32[384,768]{1,0:T(8,128)} fusion(f32[384,384]{1,0:T(8,128)S(1)} %bitcast.54, f32[384,384]{1,0:T(8,128)S(1)} %bitcast.53), kind=kLoop, calls=%fused_computation.10 | loop fusion | flops 294912 | bytes 2359296 | tf_op jit(solution)/shard_map/concatenate | solution.py:514
  102.1 0.6 copy.14
  102.8 0.6 copy.15
  (16 shorter events, 0.0 us)
Async XLA Ops:
  0.6 37.7 %copy-start = (bf16[768,384]{1,0:T(8,128)(2,1)S(1)}, bf16[768,384]{1,0:T(8,128)(2,1)}, u32[]{:S(2)}) copy-start(bf16[768,384]{1,0:T(8,128)(2,1)} %param.8) | copy-start | bytes 1769476
  0.6 0.9 copy-start.1
  1.6 0.8 copy-start.3
  2.4 0.7 copy-start.5
  3.1 35.7 %copy-start.10 = (bf16[384,768]{1,0:T(8,128)(2,1)S(1)}, bf16[384,768]{1,0:T(8,128)(2,1)}, u32[]{:S(2)}) copy-start(bf16[384,768]{1,0:T(8,128)(2,1)} %param.9) | copy-start | bytes 1769476
  39.2 1.7 %copy-start.8 = (bf16[384,256]{0,1:T(8,128)(2,1)}, bf16[384,256]{0,1:T(8,128)(2,1)S(1)}, u32[]{:S(2)}) copy-start(bf16[384,256]{0,1:T(8,128)(2,1)S(1)} %fusion.3) | copy-start | bytes 589828
  40.9 1.0 copy-start.7
  41.9 0.9 copy-start.9
  42.1 3.1 %copy-start.2 = (bf16[1,4,64,96]{3,2,1,0:T(8,128)(2,1)S(1)}, bf16[1,4,64,96]{3,2,1,0:T(8,128)(2,1)}, u32[]{:S(2)}) copy-start(bf16[1,4,64,96]{3,2,1,0:T(8,128)(2,1)} %param.5) | copy-start | bytes 147460
  42.1 3.1 %copy-start.4 = (bf16[1,4,64,96]{3,2,1,0:T(8,128)(2,1)S(1)}, bf16[1,4,64,96]{3,2,1,0:T(8,128)(2,1)}, u32[]{:S(2)}) copy-start(bf16[1,4,64,96]{3,2,1,0:T(8,128)(2,1)} %param.6) | copy-start | bytes 147460
  42.1 3.1 %copy-start.6 = (bf16[7,7,96]{2,1,0:T(8,128)(2,1)S(1)}, bf16[7,7,96]{2,1,0:T(8,128)(2,1)}, u32[]{:S(2)}) copy-start(bf16[7,7,96]{2,1,0:T(8,128)(2,1)} %refs_6_.1) | copy-start | bytes 28228

commit v5 on v4

--- a/solution.py
+++ b/solution.py
@@ -15,10 +15,16 @@
 BF16 = jnp.bfloat16
 
 
-def greet(peers):
+def mm(a, b, dims):
+    return lax.dot_general(a, b, (dims, ((), ())), preferred_element_type=F32)
+
+
+def greet(peers, between=None):
     barrier = pltpu.get_barrier_semaphore()
     for peer in peers:
         pl.semaphore_signal(barrier, inc=1, device_id=peer, device_id_type=MESH)
+    if between is not None:
+        between()
     pl.semaphore_wait(barrier, len(peers))
 
 
@@ -197,7 +203,10 @@
 
 
 def back_kernel(*refs):
-    part_out, part_norm, hat, rstd, image, grad_map, taps, pad_x, grads = refs[0:9]
+    w_in, w_out, act, d_pre, normed_all, grad_all = refs[0:6]
+    part_out, part_norm, grads = refs[52:55]
+    hat, rstd, image, grad_map, taps, pad_x = refs[6:12]
+    refs = refs[3:]
     output, grad_image, out, taps_out = refs[9:13]
     lands, msem, mrsem = refs[13:21], refs[21], refs[22]
     land, stat, csem, crsem, tall, d_conv, pad, mytaps = refs[23:31]
@@ -219,22 +228,40 @@
     y_peers = [((z * ny + k) * 2 + core, ch) for k in ys]
     z_peers = [((k * ny + y) * 2 + core, ch) for k in zs]
     stat[me] = jnp.zeros(stat.shape[1:], F32)
-    greet(peers + near + [other] + y_peers + z_peers)
+
+    def first_products():
+        part_norm[...] = (
+            mm(w_in[...], d_pre[...], ((1,), (0,))).astype(BF16).reshape(part_norm.shape)
+        )
+        normed = normed_all[...].reshape(chans, pixels)
+        grad_in = mm(normed, d_pre[...], ((1,), (1,))).astype(BF16)
+        grads[0] = grad_in.reshape(grads.shape[1:])
+
+    greet(peers + near + [other] + y_peers + z_peers, first_products)
 
     norms = [
         send(part_norm.at[peer[1]], land.at[0, d], csem.at[0, d], crsem.at[0, d], peer)
         for d, peer in enumerate(peers)
     ]
-    outs = [
-        send(part_out.at[peer[1]], land.at[1, d], csem.at[1, d], crsem.at[1, d], peer)
-        for d, peer in enumerate(peers)
-    ]
+    hidden = act.shape[0]
+    down = hidden // panel
+    for k in range(0, n, down):
+        panels = grad_all[k : k + down].reshape(hidden, pixels)
+        grad_out = mm(act[...], panels, ((1,), (1,))).astype(BF16)
+        grads[1, k : k + down] = grad_out.reshape(down, panel, hidden)
     half = ny // 2
     away = [half] + [a for d in range(half - 1, 0, -1) for a in (d, ny - d)] + [0]
     order = [lax.rem(y + a, ny) for a in away]
     firsts = [
         send(grads.at[1 - core, k], land0.at[k], ssem.at[0, d], rsem.at[0, d], other)
         for d, k in enumerate(order)
+    ]
+    part_out[...] = (
+        mm(w_out[...], act[...], ((0,), (0,))).astype(BF16).reshape(part_out.shape)
+    )
+    outs = [
+        send(part_out.at[peer[1]], land.at[1, d], csem.at[1, d], crsem.at[1, d], peer)
+        for d, peer in enumerate(peers)
     ]
     tall[...] = jnp.zeros_like(tall)
     mytaps[...] = jnp.zeros_like(mytaps)
@@ -439,30 +466,15 @@
             + [pltpu.VMEM((pixels, 128), F32), pltpu.VMEM((n, 8, pixels), F32)]
             + sems(3, n - 1),
         )(block, kernel, grad_map)
-        normed_t = normed_t.reshape(chans, pixels)
-        gall_t = gall_t.reshape(chans, pixels)
-
-        def mm(a, b, dims):
-            return lax.dot_general(a, b, (dims, ((), ())), preferred_element_type=F32)
-
-        pre = mm(w_in, normed_t, ((0,), (0,)))
+
+        pre = mm(w_in, normed_t.reshape(chans, pixels), ((0,), (0,)))
         half = 0.5 * (1.0 + jax.scipy.special.erf(pre / jnp.sqrt(2.0)))
         act = (pre * half).astype(BF16)
         slope = half + pre * jnp.exp(-0.5 * pre * pre) / jnp.sqrt(2.0 * jnp.pi)
-        d_act = mm(w_out, gall_t, ((1,), (0,)))
+        d_act = mm(w_out, gall_t.reshape(chans, pixels), ((1,), (0,)))
         d_pre = (d_act * slope).astype(BF16)
-        part_out = mm(w_out, act, ((0,), (0,))).astype(BF16)
-        part_norm = mm(w_in, d_pre, ((1,), (0,))).astype(BF16)
-        grad_in = mm(normed_t, d_pre, ((1,), (1,))).astype(BF16)
-        grad_out = mm(act, gall_t, ((1,), (1,))).astype(BF16)
-
         piece = chans // ny
-        grad_in = grad_in.reshape(ny, piece, hidden)
-        halves = [
-            grad_out[:, at : at + hidden].reshape(-1, piece, hidden)
-            for at in range(0, chans, hidden)
-        ]
-        grads = jnp.concatenate([grad_in] + halves).reshape(2, ny, piece, hidden)
+        gdims = (2, ny, piece, hidden)
         tdims = (ny, 8, 128)
         output, grad_image, total, taps_total = call(
             back_kernel,
@@ -471,7 +483,7 @@
             (
                 shape(block.shape, BF16),
                 shape(block.shape, BF16),
-                shape(grads.shape, BF16),
+                shape(gdims, BF16),
                 shape(tdims, F32),
             ),
             lands
@@ -496,17 +508,25 @@
             + sems(2, ny // 2, CHUNKS)
             + sems(ny, CHUNKS)
             + sems(2, ny // 2, CHUNKS)
-            + sems(CHUNKS, nz - 1),
+            + sems(CHUNKS, nz - 1)
+            + [
+                pltpu.VMEM(all_dims, BF16),
+                pltpu.VMEM(all_dims, BF16),
+                pltpu.VMEM(gdims, BF16),
+            ],
         )(
-            part_out.reshape(all_dims),
-            part_norm.reshape(all_dims),
+            w_in,
+            w_out,
+            act,
+            d_pre,
+            normed_t,
+            gall_t,
             hat,
             rstd,
             block,
             grad_map,
             kernel,
             pad_x,
-            grads,
         )
         total = total.astype(F32)
         grad_in = total[0].reshape(chans, hidden)

time: 104 us -> 99.6 us (0.958)
  local copies, waits for them, and re-layouts: 8.93 us -> 6.2 us
  matrix products: 3.11 us -> 1.78 us
    convert_element_type x2 -> x0, local copies, waits for them, and re-layouts: 1.33 us -> none  [the longest x1 1.16 us: shards(): part_norm = mm(w_in, d_pre, ((1,), (0,))).astype(BF16)]
    dot_general x6 -> x2, matrix products: 3.11 us -> 1.78 us  [mm(): return lax.dot_general(a, b, (dims, ((), ())), preferred_element_type=F32)]
    unnamed x24 -> x12, local copies, waits for them, and re-layouts: 5.04 us -> 4.42 us
where the time goes in v5:
time: 99.6 us; the launch traced here: 99.3 us
  Pallas kernels  89.5 us (90%)
  local copies, waits for them, and re-layouts  6.2 us (6%)
  matrix products  1.78 us (2%)
  other arithmetic  1.1 us (1%)
    pallas_call x2, Pallas kernels, run(): pl.pallas_call(body, out_shape=out_shape, in_specs=[pl.BlockSpec(memory_s...  89.5 us
    unnamed x12, local copies, waits for them, and re-layouts  4.42 us

profile of v5, /device:TPU:1, one launch (start us, length us, event | category | flops | bytes accessed | tf_op | source)
XLA Modules:
  0.0 99.3 jit_solution(2636702551833364804)
XLA Ops:
  0.6 0.0 copy-start.1
  0.6 0.0 copy-start.2
  0.7 0.9 copy-done.2
  1.5 0.0 copy-start.3
  1.5 0.8 copy-done.3
  2.4 0.0 copy-start.4
  2.4 0.7 copy-done.4
  3.1 35.2 %front.1 = (bf16[8,96,256]{2,1,0:T(8,128)(2,1)S(1)}, bf16[8,96,256]{2,1,0:T(8,128)(2,1)S(1)}, f32[96,256]{1,0:T(8,128)S(1)}, f32[1,256]{1,0:T(1,128)S(1)}, f32[10,80,96]{2,1,0:T(8,128)S(1)}) custom-call(bf16[4,64,96]{2,1,0:T(8,128)(2,1)S(1)} %bitcast.23, bf16[7,7,96]{2,1,0:T(8,128)(2,1)S(1)} %copy-done.4, bf16[4,64,96]{2,1,0:T(8,128)(2,1)S(1)} %bitcast.25), custom_call_target="tpu_custom_call" | custom-call | tf_op jit(solution)/shard_map/front/pallas_call | solution.py:46
  38.3 1.5 %multiply_convert_fusion = (bf16[384,256]{1,0:T(8,128)(2,1)S(1)}, f32[384,256]{1,0:T(8,128)S(1)}) fusion(bf16[768,256]{1,0:T(8,128)(2,1)S(1)} %bitcast.21, bf16[768,384]{1,0:T(8,128)(2,1)} %refs_0_.1), kind=kOutput, calls=%fused_computation.10 | convolution fusion | flops 151486464 | bytes 1572864 | tf_op jit(solution)/shard_map/dot_general | solution.py:19
  39.8 0.0 copy-start
  39.8 0.0 copy-done.1
  39.8 0.3 fusion.1.refs_3_
  40.1 0.7 copy-done
  40.8 54.3 %back.1 = (bf16[4,64,96]{2,1,0:T(8,128)(2,1)S(1)}, bf16[4,64,96]{2,1,0:T(8,128)(2,1)S(1)}, bf16[2,8,96,384]{3,2,1,0:T(8,128)(2,1)S(1)}, f32[8,8,128]{2,1,0:T(8,128)S(1)}) custom-call(bf16[768,384]{1,0:T(8,128)(2,1)S(1)} %copy-done, bf16[384,768]{1,0:T(8,128)(2,1)S(1)} %copy-done.1, bf16[384,256]{1,0:T(8,128)(2,1)S(1)} %get-tuple-element.25.refs_2_, ...), custom_call_target="tpu_custom_call" | custom-call | tf_op jit(solution)/shard_map/back/pallas_call | solution.py:46
  95.1 0.6 slice.15
  95.8 1.1 %slice.16 = f32[1,8,96,384]{3,2,1,0:T(8,128)} slice(bf16[2,8,96,384]{3,2,1,0:T(8,128)(2,1)S(1)} %get-tuple-element.21), slice={[0:1], [0:8], [0:96], [0:384]} | slice | bytes 2359296 | tf_op jit(solution)/shard_map/slice | solution.py:532
  96.8 0.1 fusion.6
  96.9 1.1 %pad_maximum_fusion = f32[384,768]{1,0:T(8,128)} fusion(f32[384,384]{1,0:T(8,128)S(1)} %bitcast.30, f32[384,384]{1,0:T(8,128)S(1)} %bitcast.29), kind=kLoop, calls=%fused_computation.3 | loop fusion | flops 294912 | bytes 2359296 | tf_op jit(solution)/shard_map/concatenate | solution.py:534
  98.0 0.6 copy.16
  98.7 0.6 copy.17
Async XLA Ops:
  0.6 39.1 %copy-start.1 = (bf16[384,768]{1,0:T(8,128)(2,1)S(1)}, bf16[384,768]{1,0:T(8,128)(2,1)}, u32[]{:S(2)}) copy-start(bf16[384,768]{1,0:T(8,128)(2,1)} %refs_1_.3) | copy-start | bytes 1769476
  0.6 0.9 copy-start.2
  1.5 0.8 copy-start.3
  2.4 0.7 copy-start.4
  39.8 1.1 %copy-start = (bf16[768,384]{1,0:T(8,128)(2,1)S(1)}, bf16[768,384]{1,0:T(8,128)(2,1)}, u32[]{:S(2)}) copy-start(bf16[768,384]{1,0:T(8,128)(2,1)} %refs_0_.1) | copy-start | bytes 1769476

commit v6 on v5

--- a/solution.py
+++ b/solution.py
@@ -269,9 +269,14 @@
 
     size = out.shape[2] // CHUNKS
     ring = [((z * ny + k) * 2 + core, ch) for k in (lax.rem(y + 1, ny), lax.rem(y + ny - 1, ny))]
-    for d, k in enumerate(order):
+
+    def take(d):
+        k = order[d]
         firsts[d].wait()
         mine[k] = (grads[core, k].astype(F32) + land0[k].astype(F32)).astype(BF16)
+
+    for d in range(3):
+        take(d)
     sums, moves = {}, []
     for step in range(half + 1):
         for c in range(CHUNKS):
@@ -296,6 +301,9 @@
                         sum_recv.at[way, step, c],
                         ring[way],
                     )
+            if step == 0 and c == CHUNKS - 1:
+                for d in range(3, ny):
+                    take(d)
             if step == half:
                 total = mine[y, part_rows].astype(F32)
                 for way in range(2):

time: 99.6 us -> 99.8 us (level)
  no operation moved by 1% of the time
where the time goes in v6:
time: 99.8 us; the launch traced here: 99.5 us
  Pallas kernels  89.7 us (90%)
  local copies, waits for them, and re-layouts  6.2 us (6%)
  matrix products  1.78 us (2%)
  other arithmetic  1.1 us (1%)
    pallas_call x2, Pallas kernels, run(): pl.pallas_call(body, out_shape=out_shape, in_specs=[pl.BlockSpec(memory_s...  89.7 us
    unnamed x12, local copies, waits for them, and re-layouts  4.42 us

profile of v6, /device:TPU:1, one launch (start us, length us, event | category | flops | bytes accessed | tf_op | source)
XLA Modules:
  0.0 99.5 jit_solution(5523572738881999256)
XLA Ops:
  0.6 0.0 copy-start.1
  0.6 0.0 copy-start.2
  0.7 0.9 copy-done.2
  1.5 0.0 copy-start.3
  1.5 0.8 copy-done.3
  2.4 0.0 copy-start.4
  2.4 0.7 copy-done.4
  3.1 35.2 %front.1 = (bf16[8,96,256]{2,1,0:T(8,128)(2,1)S(1)}, bf16[8,96,256]{2,1,0:T(8,128)(2,1)S(1)}, f32[96,256]{1,0:T(8,128)S(1)}, f32[1,256]{1,0:T(1,128)S(1)}, f32[10,80,96]{2,1,0:T(8,128)S(1)}) custom-call(bf16[4,64,96]{2,1,0:T(8,128)(2,1)S(1)} %bitcast.23, bf16[7,7,96]{2,1,0:T(8,128)(2,1)S(1)} %copy-done.4, bf16[4,64,96]{2,1,0:T(8,128)(2,1)S(1)} %bitcast.25), custom_call_target="tpu_custom_call" | custom-call | tf_op jit(solution)/shard_map/front/pallas_call | solution.py:46
  38.3 1.5 %multiply_convert_fusion = (bf16[384,256]{1,0:T(8,128)(2,1)S(1)}, f32[384,256]{1,0:T(8,128)S(1)}) fusion(bf16[768,256]{1,0:T(8,128)(2,1)S(1)} %bitcast.21, bf16[768,384]{1,0:T(8,128)(2,1)} %refs_0_.1), kind=kOutput, calls=%fused_computation.10 | convolution fusion | flops 151486464 | bytes 1572864 | tf_op jit(solution)/shard_map/dot_general | solution.py:19
  39.8 0.0 copy-start
  39.8 0.0 copy-done.1
  39.8 0.3 fusion.1.refs_3_
  40.1 0.7 copy-done
  40.8 54.5 %back.1 = (bf16[4,64,96]{2,1,0:T(8,128)(2,1)S(1)}, bf16[4,64,96]{2,1,0:T(8,128)(2,1)S(1)}, bf16[2,8,96,384]{3,2,1,0:T(8,128)(2,1)S(1)}, f32[8,8,128]{2,1,0:T(8,128)S(1)}) custom-call(bf16[768,384]{1,0:T(8,128)(2,1)S(1)} %copy-done, bf16[384,768]{1,0:T(8,128)(2,1)S(1)} %copy-done.1, bf16[384,256]{1,0:T(8,128)(2,1)S(1)} %get-tuple-element.25.refs_2_, ...), custom_call_target="tpu_custom_call" | custom-call | tf_op jit(solution)/shard_map/back/pallas_call | solution.py:46
  95.3 0.6 slice.15
  95.9 1.1 %slice.16 = f32[1,8,96,384]{3,2,1,0:T(8,128)} slice(bf16[2,8,96,384]{3,2,1,0:T(8,128)(2,1)S(1)} %get-tuple-element.21), slice={[0:1], [0:8], [0:96], [0:384]} | slice | bytes 2359296 | tf_op jit(solution)/shard_map/slice | solution.py:540
  97.0 0.1 fusion.6
  97.1 1.1 %pad_maximum_fusion = f32[384,768]{1,0:T(8,128)} fusion(f32[384,384]{1,0:T(8,128)S(1)} %bitcast.30, f32[384,384]{1,0:T(8,128)S(1)} %bitcast.29), kind=kLoop, calls=%fused_computation.3 | loop fusion | flops 294912 | bytes 2359296 | tf_op jit(solution)/shard_map/concatenate | solution.py:542
  98.2 0.6 copy.16
  98.8 0.6 copy.17
Async XLA Ops:
  0.6 39.1 %copy-start.1 = (bf16[384,768]{1,0:T(8,128)(2,1)S(1)}, bf16[384,768]{1,0:T(8,128)(2,1)}, u32[]{:S(2)}) copy-start(bf16[384,768]{1,0:T(8,128)(2,1)} %refs_1_.3) | copy-start | bytes 1769476
  0.6 0.9 copy-start.2
  1.5 0.8 copy-start.3
  2.4 0.7 copy-start.4
  39.8 1.1 %copy-start = (bf16[768,384]{1,0:T(8,128)(2,1)S(1)}, bf16[768,384]{1,0:T(8,128)(2,1)}, u32[]{:S(2)}) copy-start(bf16[768,384]{1,0:T(8,128)(2,1)} %refs_0_.1) | copy-start | bytes 1769476
